TPU v7x, 256 devices: a whole 4x4x8 slice. The times are simulated.
256 devices in a mesh: row: 32 (over z_lo, y, core), col: 8 (over z_hi, x).
Axes of the slice: x: 4, y: 4, z: 8 (z_hi: 2, z_lo: 4; z = z_hi * 4 + z_lo), core: 2. Of those that a mesh axis runs over, the one named last changes fastest.
Arguments:
- slab: bfloat16 [32768, 16384], P('row', 'col'), may hold values from -6 to 6
- panel_left: bfloat16 [32768, 512], P('row', 'col'), may hold values from -3 to 3
- panel_top: bfloat16 [512, 16384], P('row', 'col'), may hold values from -3 to 3
- row_bases: bfloat16 [32768, 256], P('row'), may hold values from -0.25 to 0.25
- col_bases: bfloat16 [16384, 256], P('col'), may hold values from -0.25 to 0.25
- row_ranks: int32 [64], P('row'), may hold values from 32 to 256, as said below
- col_ranks: int32 [32], P('col'), may hold values from 32 to 256, as said below
- pivot_inverse: bfloat16 [512, 512], replicated, may hold values from -0.0625 to 0.0625
- pivot_rhs: bfloat16 [512, 4096], P('row', 'col'), may hold values from -6 to 6
- rhs: bfloat16 [32768, 4096], P('row', 'col'), may hold values from -6 to 6
Outputs:
- slab_new: bfloat16 [32768, 16384], P('row', 'col')
- rhs_new: bfloat16 [32768, 4096], P('row', 'col')
Inputs may be any that keep to these rules, and one draw needn't show every extreme that they name: `row_ranks`: each entry is the rank of one tile; the value 256 occurs in every draw. `col_ranks`: each entry is the rank of one tile; the value 256 occurs in every draw.
All inputs are finite; a program needn't handle non-finite values.
Results may differ from a plain program's by a relative error of at most 0.0062.
Values may be sent and summed in bfloat16 or wider, within the bound.
No kernel may reach another device: no remote copies, remote signals or barrier semaphores. Data moves between devices by JAX's collectives and lax.ppermute only.
A program may use at most 128 MiB of HBM per device.

v0:
```python
import jax
import jax.numpy as jnp
from jax import lax
from jax.sharding import PartitionSpec as P


def from_everyone(array, axis):
    copies = jnp.broadcast_to(array, (lax.axis_size(axis), *array.shape))
    return lax.all_to_all(copies, axis, split_axis=0, concat_axis=0, tiled=True)


def joined_along(blocks, dim):
    blocks = jnp.moveaxis(blocks, 0, dim)
    lengths = blocks.shape
    return blocks.reshape(*lengths[:dim], lengths[dim] * lengths[dim + 1], *lengths[dim + 2 :])


def gather_directly(array, axis, dim):
    blocks = from_everyone(array, axis)
    return joined_along(blocks, dim)


def per_device(
    slab,
    panel_left,
    panel_top,
    row_bases,
    col_bases,
    row_ranks,
    col_ranks,
    pivot_inverse,
    pivot_rhs,
    rhs,
):
    tile_order = pivot_inverse.shape[0]
    rank_width = row_bases.shape[1]
    row_count = row_ranks.shape[0]
    column_count = col_ranks.shape[0]
    gain_width = rhs.shape[1]
    levels = jnp.arange(rank_width, dtype=jnp.int32)
    keep_row = (levels[None, :] < row_ranks[:, None]).astype(jnp.float32)
    keep_column = (levels[None, :] < col_ranks[:, None]).astype(jnp.float32)
    left_bases = row_bases.reshape(row_count, tile_order, rank_width)
    right_bases = col_bases.reshape(column_count, tile_order, rank_width)
    left_tiles = panel_left.reshape(row_count, tile_order, panel_left.shape[1])
    part_core = jnp.einsum(
        "tbr,tbc->trc", left_bases, left_tiles, preferred_element_type=jnp.float32
    )
    part_core = (part_core * keep_row[:, :, None]).astype(jnp.bfloat16)
    row_core = gather_directly(part_core, "col", 2)
    shaped = panel_top.reshape(panel_top.shape[0], column_count, tile_order)
    projected = jnp.einsum("pjc,jcr->pjr", shaped, right_bases, preferred_element_type=jnp.float32)
    outgoing = (projected * keep_column[None]).astype(jnp.bfloat16)
    arrived, rhs_rows = (
        lax.all_gather(outgoing, "row", axis=0, tiled=True),
        lax.all_gather(pivot_rhs, "row", axis=0, tiled=True),
    )
    solved = jnp.dot(pivot_inverse, rhs_rows, preferred_element_type=jnp.float32)
    core_block = jnp.einsum(
        "irp,pjs->ijrs", row_core, arrived, preferred_element_type=jnp.float32
    ).astype(jnp.bfloat16)
    spread = jnp.einsum(
        "ibr,ijrs->ijbs", left_bases, core_block, preferred_element_type=jnp.float32
    ).astype(jnp.bfloat16)
    change = jnp.einsum("ijbs,jcs->ibjc", spread, right_bases, preferred_element_type=jnp.float32)
    change = change.reshape(row_count * tile_order, column_count * tile_order)
    slab_new = (slab.astype(jnp.float32) - change).astype(jnp.bfloat16)
    pivot_solution = solved.astype(jnp.bfloat16)
    reduced = jnp.einsum(
        "irp,pg->irg", row_core, pivot_solution, preferred_element_type=jnp.float32
    ).astype(jnp.bfloat16)
    lowered = jnp.einsum("ibr,irg->ibg", left_bases, reduced, preferred_element_type=jnp.float32)
    lowered = lowered.reshape(row_count * tile_order, gain_width)
    rhs_new = (rhs.astype(jnp.float32) - lowered).astype(jnp.bfloat16)
    return (slab_new, rhs_new)


def solution(mesh):
    in_specs = (
        P("row", "col"),
        P("row", "col"),
        P("row", "col"),
        P("row", None),
        P("col", None),
        P("row"),
        P("col"),
        P(),
        P("row", "col"),
        P("row", "col"),
    )
    out_specs = (P("row", "col"), P("row", "col"))
    return jax.shard_map(
        per_device, mesh=mesh, in_specs=in_specs, out_specs=out_specs, check_vma=False
    )
```

profile of v0, /device:TPU:1, one launch (start us, length us, event | category | flops | bytes accessed | tf_op | source)
XLA Modules:
  0.0 118.2 jit_solution(15169704312447534713)
XLA Ops:
  7.2 0.0 copy-start
  7.2 0.0 copy-start.2
  7.2 0.0 all-gather.2.cloned.1.call-start
  7.2 0.8 fusion.16
  8.1 0.3 copy-done
  8.4 1.1 fusion.10
  9.5 0.6 copy.17
  10.1 0.0 all-gather.2.cloned.1.call-update
  10.1 0.7 compare_convert_fusion
  10.9 1.3 %fusion.8 = bf16[2,256,64]{1,2,0:T(8,128)(2,1)S(1)} fusion(bf16[2,512,256]{2,1,0:T(8,128)(2,1)} %bitcast.57, bf16[8,2,8,512]{3,2,1,0:T(8,128)(2,1)} %bitcast.62, f32[2,256]{1,0:T(2,128)S(1)} %compare_convert_fusion), kind=kOutput, calls=%fused_computation.14 | convolution fusion | flops 33619968 | bytes 722944 | tf_op jit(solution)/shard_map/tbr,tbc->trc/dot_general | solution.py:46
  12.2 0.8 broadcast_in_dim.2
  13.0 11.5 %all-to-all-start = ((bf16[8,2,256,64]{2,3,1,0:T(8,128)(2,1)}), bf16[8,2,256,64]{2,3,1,0:T(8,128)(2,1)S(1)}, u32[]{:S(2)}, u32[]{:S(2)}) async-start(bf16[8,2,256,64]{2,3,1,0:T(8,128)(2,1)} %broadcast_in_dim.2), calls=%async_computation | async-start | bytes 1048576 | tf_op jit(solution)/shard_map/all_to_all | solution.py:9
  24.5 46.1 %all_gather.7 = bf16[512,512]{1,0:T(8,128)(2,1)S(1)} all-gather(bf16[16,512]{1,0:T(8,128)(2,1)} %param.18), channel_id=1, replica_groups=mesh['row'=32,'col'=8] {'row'}, dimensions={0}, use_global_device_ids=true | all-gather | bytes 540672 | tf_op jit(solution)/shard_map/all_gather | solution.py:56
  70.6 0.0 copy-done.2
  70.6 1.3 %fusion.6 = bf16[512,512,1]{1,0,2:T(8,128)(2,1)} fusion(bf16[512,512]{1,0:T(8,128)(2,1)S(1)} %copy-done.2, bf16[512,512]{1,0:T(8,128)(2,1)S(1)} %all_gather.7), kind=kOutput, calls=%fused_computation.11 | convolution fusion | flops 268697600 | bytes 1572864 | tf_op jit(solution)/shard_map/dot_general | solution.py:58
  71.9 0.0 all-to-all-done
  71.9 0.8 copy.19
  72.7 2.2 %fusion.7 = f32[2,512,512]{1,2,0:T(8,128)S(1)} fusion(bf16[2,512,256]{2,1,0:T(8,128)(2,1)} %bitcast.58, bf16[2,256,512]{1,2,0:T(8,128)(2,1)} %bitcast.60, bf16[512,512,1]{1,0,2:T(8,128)(2,1)} %fusion.6), kind=kOutput, calls=%fused_computation.12 | convolution fusion | flops 537133056 | bytes 3670016 | tf_op jit(solution)/shard_map/ibr,irg->ibg/dot_general | solution.py:72
  74.9 2.7 %fusion = bf16[1024,512]{1,0:T(8,128)(2,1)} fusion(f32[2,512,512]{1,2,0:T(8,128)S(1)} %fusion.7, bf16[1024,512]{1,0:T(8,128)(2,1)} %param.19), kind=kLoop, calls=%fused_computation.3 | loop fusion | flops 1572864 | bytes 4194304 | tf_op jit(solution)/shard_map/convert_element_type | solution.py:74
  77.6 2.1 %all-gather.2.cloned.1.call-done = bf16[512,4,256]{2,1,0:T(4,128)(2,1)} async-done(((bf16[16,4,256]{2,1,0:T(4,128)(2,1)}), bf16[512,4,256]{2,1,0:T(4,128)(2,1)}) %all-gather.2.cloned.1.call-update) | async-done | bytes 1048592 | tf_op jit(solution)/shard_map/all_gather | solution.py:55
  79.8 2.1 %fusion.5 = bf16[2,4,256,256]{2,3,0,1:T(8,128)(2,1)S(1)} fusion(bf16[2,256,512,1]{1,2,0,3:T(8,128)(2,1)} %bitcast.61, bf16[512,4,256,1]{2,1,0,3:T(4,128)(2,1)} %bitcast.64), kind=kOutput, calls=%fused_computation.8 | convolution fusion | flops 537395200 | bytes 2621440 | tf_op jit(solution)/shard_map/irp,pjs->ijrs/dot_general | solution.py:59
  81.9 6.1 %convolution_bitcast_fusion = f32[2,512,4,512]{3,1,0,2:T(8,128)} fusion(bf16[4,512,256,1]{2,1,3,0:T(8,128)(2,1)S(1)} %bitcast.53, bf16[2,4,256,256]{2,3,0,1:T(8,128)(2,1)S(1)} %fusion.5, bf16[2,512,256,1]{2,1,0,3:T(8,128)(2,1)} %bitcast.59), kind=kOutput, calls=%fused_computation.1 | convolution fusion | flops 1611661312 | bytes 11010048 | tf_op jit(solution)/shard_map/ijbs,jcs->ibjc/dot_general | solution.py:65
  88.0 12.0 %copy.23 = f32[2,512,4,512]{3,2,1,0:T(4,128)} copy(f32[2,512,4,512]{3,1,0,2:T(8,128)} %convolution_bitcast_fusion) | data formatting | bytes 16777216 | tf_op jit(solution)/shard_map/ijbs,jcs->ibjc/transpose | solution.py:65
  100.0 0.0 copy-start.1
  100.0 7.8 %copy.35 = f32[128,8,4,512]{3,1,2,0:T(8,128)S(1)} copy(f32[128,8,4,512]{3,2,1,0:T(4,128)} %bitcast.55) | data formatting | bytes 16777216
  107.8 0.0 copy-done.1
  107.8 3.5 %subtract_convert_fusion = bf16[1024,2048]{1,0:T(8,128)(2,1)} fusion(f32[1024,2048]{1,0:T(8,128)S(1)} %bitcast.56, bf16[1024,2048]{1,0:T(8,128)(2,1)S(1)} %copy-done.1), kind=kLoop, calls=%fused_computation | loop fusion | flops 6291456 | bytes 16777216 | tf_op jit(solution)/shard_map/convert_element_type | solution.py:67
Async XLA Ops:
  7.2 1.2 %copy-start = (bf16[2048,256]{1,0:T(8,128)(2,1)S(1)}, bf16[2048,256]{1,0:T(8,128)(2,1)}, u32[]{:S(2)}) copy-start(bf16[2048,256]{1,0:T(8,128)(2,1)} %param.14) | copy-start | bytes 3145732
  7.2 63.5 %copy-start.2 = (bf16[512,512]{1,0:T(8,128)(2,1)S(1)}, bf16[512,512]{1,0:T(8,128)(2,1)}, u32[]{:S(2)}) copy-start(bf16[512,512]{1,0:T(8,128)(2,1)} %param.17) | copy-start | bytes 1572868
  7.2 72.6 %all-gather.2.cloned.1.call-start = ((), (), s32[]{:S(2)}) async-start(), calls=%async_computation.1 | async-start | bytes 1081344 | tf_op jit(solution)/shard_map/all_gather | solution.py:55
  13.0 58.9 %all-to-all-start = ((bf16[8,2,256,64]{2,3,1,0:T(8,128)(2,1)}), bf16[8,2,256,64]{2,3,1,0:T(8,128)(2,1)S(1)}, u32[]{:S(2)}, u32[]{:S(2)}) async-start(bf16[8,2,256,64]{2,3,1,0:T(8,128)(2,1)} %broadcast_in_dim.2), calls=%async_computation | async-start | bytes 1048576 | tf_op jit(solution)/shard_map/all_to_all | solution.py:9
  100.0 7.9 %copy-start.1 = (bf16[1024,2048]{1,0:T(8,128)(2,1)S(1)}, bf16[1024,2048]{1,0:T(8,128)(2,1)}, u32[]{:S(2)}) copy-start(bf16[1024,2048]{1,0:T(8,128)(2,1)} %param.10) | copy-start | bytes 12582916
Sparse Core Ops, SparseCore 0:
  10.3 69.4 all-gather.1
where the time goes:
time: 119 us; the launch traced here: 118 us
  blocking collectives  46.1 us (39%)
  local copies, waits for them, and re-layouts  22.5 us (19%)
  matrix products  14.1 us (12%)
  between operations  14.1 us (12%)
  starting transfers between devices  11.5 us (10%)
  other arithmetic  7.77 us (7%)
  waiting for transfers between devices  2.16 us (2%)
    all_gather x1, blocking collectives, per_device(): lax.all_gather(pivot_rhs, 'row', axis=0, tiled=True)  46.1 us
    transpose x1, local copies, waits for them, and re-layouts, per_device(): jnp.einsum('ijbs,jcs->ibjc', spread, right_bases, preferred_element_type=...  12 us
    all_to_all x1, starting transfers between devices, from_everyone(): return lax.all_to_all(copies, axis, split_axis=0, concat_axis=0, tiled=True)  11.5 us
    unnamed x7, local copies, waits for them, and re-layouts  8.2 us
    dot_general x1, matrix products, per_device(): jnp.einsum('ijbs,jcs->ibjc', spread, right_bases, preferred_element_type=...  6.11 us
    convert_element_type x1, other arithmetic, per_device(): slab_new = (slab.astype(jnp.float32) - change).astype(jnp.bfloat16)  3.5 us
    convert_element_type x1, other arithmetic, per_device(): rhs_new = (rhs.astype(jnp.float32) - lowered).astype(jnp.bfloat16)  2.7 us
  transfers between devices with their start and end apart: 2, of which 1 were waited for; matrix products, arithmetic and copies ran while one was open for 8% of the time, Pallas kernels for 0%

commit v1 on v0

v1 whole, which is shorter than its diff:
```python
import jax
import jax.numpy as jnp
from jax import lax
from jax.experimental import pallas as pl
from jax.experimental.pallas import tpu as pltpu
from jax.sharding import PartitionSpec as P


ROW, COL = 32, 8
BF = jnp.bfloat16
F32 = jnp.float32
VMEM = pl.BlockSpec(memory_space=pltpu.VMEM)
SMEM = pl.BlockSpec(memory_space=pltpu.SMEM)
ANY = pl.BlockSpec(memory_space=pl.ANY)
HBM = pl.BlockSpec(memory_space=pltpu.HBM)


def dot(a, b):
    return lax.dot_general(a, b, (((1,), (0,)), ((), ())), preferred_element_type=F32)


def dot_t(a, b):
    return lax.dot_general(a, b, (((1,), (1,)), ((), ())), preferred_element_type=F32)


def exchange(array, zl=0, y=0, core=0, zh=0, x=0):
    row_bits = zl * 8 + y * 2 + core
    col_bits = zh * 4 + x
    pairs = [
        (r * COL + c, (r ^ row_bits) * COL + (c ^ col_bits)) for r in range(ROW) for c in range(COL)
    ]
    return lax.ppermute(array, ("row", "col"), pairs)


def grant(mib):
    return pltpu.CompilerParams(vmem_limit_bytes=mib << 20)


def cost(flops, bytes_accessed):
    return pl.CostEstimate(flops=flops, bytes_accessed=bytes_accessed, transcendentals=0)


def project_kernel(
    row_ranks_h, col_ranks_h, left_t, bases, top, right, pivot,
    kt_ref, pack_ref, lt_v, bases_v, top_v, right_v, row_ranks, col_ranks, sems,
):
    tile = 512
    sources = [(top, top_v), (left_t, lt_v), (pivot, pack_ref.at[:, 1024:])]
    sources += [(right.at[j * tile : (j + 1) * tile], right_v.at[j * tile : (j + 1) * tile]) for j in range(4)]
    sources += [(bases.at[i * tile : (i + 1) * tile], bases_v.at[i * tile : (i + 1) * tile]) for i in range(2)]
    sources += [(col_ranks_h, col_ranks), (row_ranks_h, row_ranks)]
    copies = [pltpu.make_async_copy(a, b, sems.at[n]) for n, (a, b) in enumerate(sources)]
    for copy in copies:
        copy.start()
    copies[9].wait()
    copies[10].wait()
    lane = lax.broadcasted_iota(jnp.int32, (16, 256), 1)
    copies[0].wait()
    for j in range(4):
        copies[3 + j].wait()
        part = dot(top_v[:, j * tile : (j + 1) * tile], right_v[j * tile : (j + 1) * tile, :])
        part = jnp.where(lane < col_ranks[j], part, 0.0)
        pack_ref[:, j * 256 : (j + 1) * 256] = part.astype(BF)
    lane = lax.broadcasted_iota(jnp.int32, (64, 256), 1)
    copies[1].wait()
    for i in range(2):
        copies[7 + i].wait()
        part = dot(lt_v[:, i * tile : (i + 1) * tile], bases_v[i * tile : (i + 1) * tile, :])
        part = jnp.where(lane < row_ranks[i], part, 0.0)
        kt_ref[:, i * 256 : (i + 1) * 256] = part.astype(BF)
    copies[2].wait()


def project(row_ranks, col_ranks, left_t, bases, top, right, pivot):
    return pl.pallas_call(
        project_kernel,
        out_shape=(
            jax.ShapeDtypeStruct((64, 512), BF),
            jax.ShapeDtypeStruct((16, 1536), BF),
        ),
        in_specs=[HBM] * 7,
        out_specs=(VMEM, VMEM),
        scratch_shapes=[
            pltpu.VMEM((64, 1024), BF),
            pltpu.VMEM((1024, 256), BF),
            pltpu.VMEM((16, 2048), BF),
            pltpu.VMEM((2048, 256), BF),
            pltpu.SMEM((2,), jnp.int32),
            pltpu.SMEM((4,), jnp.int32),
            pltpu.SemaphoreType.DMA((11,)),
        ],
        compiler_params=grant(8),
        cost_estimate=cost(50_000_000, 1_800_000),
        name="project",
    )(*(in_hbm(a) for a in (row_ranks, col_ranks, left_t, bases, top, right, pivot)))


def in_hbm(array):
    return pltpu.with_memory_space_constraint(array, pltpu.HBM)


def load_kernel(after, *refs):
    del after
    count = (len(refs) - 1) // 2
    sems = refs[-1]
    copies = [pltpu.make_async_copy(refs[n], refs[count + n], sems.at[n]) for n in range(count)]
    for copy in copies:
        copy.start()
    for copy in copies:
        copy.wait()


def load(after, *arrays):
    return pl.pallas_call(
        load_kernel,
        out_shape=tuple(jax.ShapeDtypeStruct(a.shape, a.dtype) for a in arrays),
        in_specs=[ANY] + [HBM] * len(arrays),
        out_specs=(VMEM,) * len(arrays),
        scratch_shapes=[pltpu.SemaphoreType.DMA((len(arrays),))],
        compiler_params=grant(10),
        cost_estimate=cost(0, 14_000_000),
        name="load",
    )(after, *(in_hbm(a) for a in arrays))


def join_kernel(p0, p1, p2, p3, k0, k1, m_ref, k_ref):
    for n, piece in enumerate((p0, p1, p2, p3)):
        m_ref[n * 16 : (n + 1) * 16, :] = piece[...]
    k_ref[:64, :] = k0[...]
    k_ref[64:, :] = k1[...]


def join(packs, parts):
    return pl.pallas_call(
        join_kernel,
        out_shape=(
            jax.ShapeDtypeStruct((64, 1536), BF),
            jax.ShapeDtypeStruct((128, 512), BF),
        ),
        in_specs=[VMEM] * 6,
        out_specs=(VMEM,) * 2,
        compiler_params=grant(6),
        cost_estimate=cost(0, 700_000),
        name="join",
    )(*packs, *parts)


def place():
    r = lax.axis_index("row")
    c = lax.axis_index("col")
    return r // 8, (r // 2) % 4, r % 2, c // 4, c % 4


def blocks():
    zl, y, core, zh, x = place()
    n = 0
    for half in range(2):
        for dy in range(4):
            for dz in range(4):
                z_from, y_from, core_from = zl ^ dz, y ^ dy, core ^ half
                natural = (z_from * 4 + y_from) * 32 + core_from * 16
                col_from = z_from * 2 + y_from // 2
                stacked = (
                    ((col_from % 4) ^ x) * 128
                    + ((col_from // 4) ^ zh) * 64
                    + (y_from % 2) * 32
                    + core_from * 16
                )
                yield n * 16, pl.multiple_of(natural, 16), pl.multiple_of(stacked, 16)
                n += 1


def left_kernel(k0, k1, k2, k3, bases, g_ref, stack, ordered):
    for n, piece in enumerate((k0, k1, k2, k3)):
        stack[n * 128 : (n + 1) * 128, :] = piece[...]
    for at, _, stacked in blocks():
        ordered[at : at + 16, :] = stack[pl.ds(stacked, 16), :]
    for i in range(2):
        rows = slice(i * 512, (i + 1) * 512)
        g_ref[rows, :] = dot_t(bases[rows, :], ordered[:, i * 256 : (i + 1) * 256]).astype(BF)


def left_product(parts, bases):
    return pl.pallas_call(
        left_kernel,
        out_shape=jax.ShapeDtypeStruct((1024, 512), BF),
        in_specs=[VMEM] * 5,
        out_specs=VMEM,
        scratch_shapes=[pltpu.VMEM((512, 512), BF), pltpu.VMEM((512, 512), BF)],
        cost_estimate=cost(270_000_000, 2_000_000),
        compiler_params=grant(10),
        name="left_product",
    )(*parts, bases)


def update_kernel(g, p0, p1, p2, p3, p4, p5, p6, p7, right, slab, rhs, inverse, slab_out, rhs_out, wide, slab_v, rhs_v, natural, solved, ordered, sems):
    pieces = (p0, p1, p2, p3, p4, p5, p6, p7)
    tile = 512
    for j in range(4):
        core = jnp.concatenate([p[:, j * 256 : (j + 1) * 256] for p in pieces], axis=0)
        for i in range(2):
            rows = slice(i * tile, (i + 1) * tile)
            wide[j, rows, :] = dot(g[rows, :], core).astype(BF)
    copies = []
    for j in range(4):
        cols = slice(j * tile, (j + 1) * tile)
        change = dot_t(wide[j], right[cols, :])
        slab_v[:, cols] = (slab[:, cols].astype(F32) - change).astype(BF)
        copies.append(pltpu.make_async_copy(slab_v.at[:, cols], slab_out.at[:, cols], sems.at[j]))
        copies[-1].start()
    for at, to, _ in blocks():
        natural[pl.ds(to, 16), :] = pieces[at // 64][at % 64 : at % 64 + 16, 1024:]
    solved[...] = dot(inverse[...], natural[...]).astype(BF)
    for at, to, _ in blocks():
        ordered[at : at + 16, :] = solved[pl.ds(to, 16), :]
    for i in range(2):
        rows = slice(i * tile, (i + 1) * tile)
        rhs_v[rows, :] = (rhs[rows, :].astype(F32) - dot(g[rows, :], ordered[...])).astype(BF)
        copies.append(pltpu.make_async_copy(rhs_v.at[rows], rhs_out.at[rows], sems.at[4 + i]))
        copies[-1].start()
    for copy in copies:
        copy.wait()


def update(g, pieces, right, slab, rhs, inverse):
    return pl.pallas_call(
        update_kernel,
        out_shape=(
            jax.ShapeDtypeStruct((1024, 2048), BF),
            jax.ShapeDtypeStruct((1024, 512), BF),
        ),
        in_specs=[VMEM] * 13,
        out_specs=(HBM, HBM),
        scratch_shapes=[
            pltpu.VMEM((4, 1024, 256), BF),
            pltpu.VMEM((1024, 2048), BF),
            pltpu.VMEM((1024, 512), BF),
            pltpu.VMEM((512, 512), BF),
            pltpu.VMEM((512, 512), BF),
            pltpu.VMEM((512, 512), BF),
            pltpu.SemaphoreType.DMA((6,)),
        ],
        compiler_params=grant(28),
        cost_estimate=cost(3_000_000_000, 16_000_000),
        name="update",
    )(g, *pieces, right, slab, rhs, inverse)


def per_device(
    slab,
    panel_left,
    panel_top,
    row_bases,
    col_bases,
    row_ranks,
    col_ranks,
    pivot_inverse,
    pivot_rhs,
    rhs,
):
    part, pack = project(
        row_ranks, col_ranks, panel_left.T, row_bases, panel_top, col_bases, pivot_rhs
    )
    part_far = exchange(part, zh=1)
    packs = [pack] + [exchange(pack, zl=d) for d in (1, 2, 3)]
    bases, right, slab, rhs, inverse = load(
        pack, row_bases, col_bases, slab, rhs, pivot_inverse
    )
    piece, left_part = join(packs, (part, part_far))
    pieces = [piece] + [exchange(piece, y=d) for d in (1, 2, 3)]
    lefts = [left_part] + [exchange(left_part, x=d) for d in (1, 2, 3)]
    pieces += [exchange(p, core=1) for p in pieces]
    g = left_product(lefts, bases)
    return update(g, pieces, right, slab, rhs, inverse)


def solution(mesh):
    in_specs = (
        P("row", "col"),
        P("row", "col"),
        P("row", "col"),
        P("row", None),
        P("col", None),
        P("row"),
        P("col"),
        P(),
        P("row", "col"),
        P("row", "col"),
    )
    out_specs = (P("row", "col"), P("row", "col"))
    return jax.shard_map(
        per_device, mesh=mesh, in_specs=in_specs, out_specs=out_specs, check_vma=False
    )
```

time: 119 us -> 43.1 us (0.36)
  blocking collectives: 46.1 us -> 0 us
  local copies, waits for them, and re-layouts: 22.5 us -> 0 us
  matrix products: 14.1 us -> 0 us
  between operations: 14.1 us -> 0.7 us
  Pallas kernels: 0 us -> 10.3 us
  starting transfers between devices: 11.5 us -> 21.3 us
  waiting for transfers between devices: 2.16 us -> 10.6 us
  other arithmetic: 7.77 us -> 0 us
    all_gather x1 -> x0, blocking collectives: 46.1 us -> none  [per_device(): lax.all_gather(pivot_rhs, 'row', axis=0, tiled=True)]
    ppermute x0 -> x14, starting transfers between devices: none -> 21.3 us  [exchange(): return lax.ppermute(array, ('row', 'col'), pairs)]
    dot_general x6 -> x0, matrix products: 14.1 us -> none  [the longest x1 6.11 us: per_device(): jnp.einsum('ijbs,jcs->ibjc', spread, right_bases, preferred_element_type=...]
    transpose x1 -> x0, local copies, waits for them, and re-layouts: 12 us -> none  [per_device(): jnp.einsum('ijbs,jcs->ibjc', spread, right_bases, preferred_element_type=...]
    all_to_all x1 -> x0, starting transfers between devices: 11.5 us -> none  [from_everyone(): return lax.all_to_all(copies, axis, split_axis=0, concat_axis=0, tiled=True)]
    ppermute x0 -> x14, waiting for transfers between devices: none -> 10.6 us  [exchange(): return lax.ppermute(array, ('row', 'col'), pairs)]
    pallas_call x0 -> x5, Pallas kernels: none -> 10.3 us  [the longest x1 4.33 us: update(): pl.pallas_call(update_kernel, out_shape=(jax.ShapeDtypeStruct((1024, 2048...]
    unnamed x7 -> x0, local copies, waits for them, and re-layouts: 8.2 us -> none
  transfers between devices with their start and end apart: 2 -> 14, of which waited for: 1 -> 4; matrix products, arithmetic and copies ran while one was open for 8% -> 0% of each run, Pallas kernels for 0% -> 9%
where the time goes in v1:
time: 43.1 us; the launch traced here: 42.9 us
  starting transfers between devices  21.3 us (49%)
  waiting for transfers between devices  10.6 us (25%)
  Pallas kernels  10.3 us (24%)
  between operations  0.7 us (2%)
    ppermute x14, starting transfers between devices, exchange(): return lax.ppermute(array, ('row', 'col'), pairs)  21.3 us
    ppermute x14, waiting for transfers between devices, exchange(): return lax.ppermute(array, ('row', 'col'), pairs)  10.6 us
    pallas_call x1, Pallas kernels, update(): pl.pallas_call(update_kernel, out_shape=(jax.ShapeDtypeStruct((1024, 2048...  4.33 us
    pallas_call x1, Pallas kernels, load(): pl.pallas_call(load_kernel, out_shape=tuple((jax.ShapeDtypeStruct(a.shape...  3.08 us
    pallas_call x1, Pallas kernels, project(): pl.pallas_call(project_kernel, out_shape=(jax.ShapeDtypeStruct((64, 512),...  2.32 us
  transfers between devices with their start and end apart: 14, of which 4 were waited for; matrix products, arithmetic and copies ran while one was open for 0% of the time, Pallas kernels for 9%

profile of v1, /device:TPU:1, one launch (start us, length us, event | category | flops | bytes accessed | tf_op | source)
XLA Modules:
  0.0 42.9 jit_solution(2278708348448032453)
XLA Ops:
  0.6 2.3 %project.1 = (bf16[64,512]{1,0:T(8,128)(2,1)S(1)}, bf16[16,1536]{1,0:T(8,128)(2,1)S(1)}) custom-call(s32[2]{0:T(128)} %row_ranks_h.1, s32[4]{0:T(128)} %col_ranks_h.1, bf16[64,1024]{1,0:T(8,128)(2,1)} %bitcast.1, bf16[1024,256]{1,0:T(8,128)(2,1)} %refs_0_.1, bf16[16,2048]{1,0:T(8,128)(2,1)} %top.1, bf16[2048,256]{1,0:T(8,128)(2,1)} %refs_1_.1, ...), custom_call_target="tpu_custom_call" | custom-call | flops 50000000 | bytes 1800000 | tf_op jit(solution)/shard_map/project/pallas_call | solution.py:75
  3.0 7.8 %collective-permute-start.3 = (bf16[64,512]{1,0:T(8,128)(2,1)S(1)}, bf16[64,512]{1,0:T(8,128)(2,1)S(1)}, u32[]{:S(2)}, u32[]{:S(2)}) collective-permute-start(bf16[64,512]{1,0:T(8,128)(2,1)S(1)} %get-tuple-element.12.k0), channel_id=1, source_target_pairs={{0,4},{1,5},{2,6},{3,7},{4,0},{5,1},{6,2},{7,3},{8,12},{9,13},{10,... | collective-permute-start | bytes 196616 | tf_op jit(solution)/shard_map/ppermute | solution.py:32
  10.8 1.6 %collective-permute-start.2 = (bf16[16,1536]{1,0:T(8,128)(2,1)S(1)}, bf16[16,1536]{1,0:T(8,128)(2,1)S(1)}, u32[]{:S(2)}, u32[]{:S(2)}) collective-permute-start(bf16[16,1536]{1,0:T(8,128)(2,1)S(1)} %get-tuple-element.11.p0.after), channel_id=1, source_target_pairs={{0,192},{1,193},{2,194},{3,195},{4,196},{5,197},{6,198},{7,199},{8... | collective-permute-start | bytes 147464 | tf_op jit(solution)/shard_map/ppermute | solution.py:32
  12.4 0.3 collective-permute-start.1
  12.7 1.6 %collective-permute-start = (bf16[16,1536]{1,0:T(8,128)(2,1)S(1)}, bf16[16,1536]{1,0:T(8,128)(2,1)S(1)}, u32[]{:S(2)}, u32[]{:S(2)}) collective-permute-start(bf16[16,1536]{1,0:T(8,128)(2,1)S(1)} %get-tuple-element.11.p0.after), channel_id=1, source_target_pairs={{0,64},{1,65},{2,66},{3,67},{4,68},{5,69},{6,70},{7,71},{8,72},{9,... | collective-permute-start | bytes 147464 | tf_op jit(solution)/shard_map/ppermute | solution.py:32
  14.3 1.5 %collective-permute-done.2.p3 = bf16[16,1536]{1,0:T(8,128)(2,1)S(1)} collective-permute-done((bf16[16,1536]{1,0:T(8,128)(2,1)S(1)}, bf16[16,1536]{1,0:T(8,128)(2,1)S(1)}, u32[]{:S(2)}, u32[]{:S(2)}) %collective-permute-start.2) | collective-permute-done | bytes 49184 | tf_op jit(solution)/shard_map/ppermute | solution.py:32
  15.8 3.8 %collective-permute-done.1.p2 = bf16[16,1536]{1,0:T(8,128)(2,1)S(1)} collective-permute-done((bf16[16,1536]{1,0:T(8,128)(2,1)S(1)}, bf16[16,1536]{1,0:T(8,128)(2,1)S(1)}, u32[]{:S(2)}, u32[]{:S(2)}) %collective-permute-start.1) | collective-permute-done | bytes 49184 | tf_op jit(solution)/shard_map/ppermute | solution.py:32
  19.6 0.0 collective-permute-done.p1
  19.6 0.0 collective-permute-done.3.k1
  19.6 2.8 %collective-permute-start.9 = (bf16[64,1536]{1,0:T(8,128)(2,1)S(1)}, bf16[64,1536]{1,0:T(8,128)(2,1)S(1)}, u32[]{:S(2)}, u32[]{:S(2)}) collective-permute-start(bf16[64,1536]{1,0:T(8,128)(2,1)S(1)} %get-tuple-element.15.p0), channel_id=1, source_target_pairs={{0,48},{1,49},{2,50},{3,51},{4,52},{5,53},{6,54},{7,55},{8,56},{9,... | collective-permute-start | bytes 589832 | tf_op jit(solution)/shard_map/ppermute | solution.py:32
  22.4 0.3 collective-permute-start.8
  22.8 0.3 collective-permute-start.7
  23.1 2.5 %collective-permute-start.6 = (bf16[128,512]{1,0:T(8,128)(2,1)S(1)}, bf16[128,512]{1,0:T(8,128)(2,1)S(1)}, u32[]{:S(2)}, u32[]{:S(2)}) collective-permute-start(bf16[128,512]{1,0:T(8,128)(2,1)S(1)} %get-tuple-element.13.k0), channel_id=1, source_target_pairs={{0,3},{1,2},{2,1},{3,0},{4,7},{5,6},{6,5},{7,4},{8,11},{9,10},{10,... | collective-permute-start | bytes 393224 | tf_op jit(solution)/shard_map/ppermute | solution.py:32
  25.6 0.5 %collective-permute-start.5 = (bf16[128,512]{1,0:T(8,128)(2,1)S(1)}, bf16[128,512]{1,0:T(8,128)(2,1)S(1)}, u32[]{:S(2)}, u32[]{:S(2)}) collective-permute-start(bf16[128,512]{1,0:T(8,128)(2,1)S(1)} %get-tuple-element.13.k0), channel_id=1, source_target_pairs={{0,2},{1,3},{2,0},{3,1},{4,6},{5,7},{6,4},{7,5},{8,10},{9,11},{10,... | collective-permute-start | bytes 393224 | tf_op jit(solution)/shard_map/ppermute | solution.py:32
  26.1 4.9 %collective-permute-done.6.k3 = bf16[128,512]{1,0:T(8,128)(2,1)S(1)} collective-permute-done((bf16[128,512]{1,0:T(8,128)(2,1)S(1)}, bf16[128,512]{1,0:T(8,128)(2,1)S(1)}, u32[]{:S(2)}, u32[]{:S(2)}) %collective-permute-start.6) | collective-permute-done | bytes 131104 | tf_op jit(solution)/shard_map/ppermute | solution.py:32
  30.9 1.1 %collective-permute-start.10 = (bf16[64,1536]{1,0:T(8,128)(2,1)S(1)}, bf16[64,1536]{1,0:T(8,128)(2,1)S(1)}, u32[]{:S(2)}, u32[]{:S(2)}) collective-permute-start(bf16[64,1536]{1,0:T(8,128)(2,1)S(1)} %get-tuple-element.15.p0), channel_id=1, source_target_pairs={{0,8},{1,9},{2,10},{3,11},{4,12},{5,13},{6,14},{7,15},{8,0},{9,1},... | collective-permute-start | bytes 589832 | tf_op jit(solution)/shard_map/ppermute | solution.py:32
  32.1 0.0 collective-permute-done.9.p3
  32.1 0.4 collective-permute-start.13
  32.5 0.0 collective-permute-done.8.p2
  32.5 0.1 collective-permute-start.12
  32.6 0.0 collective-permute-done.7.p1
  32.6 0.6 %collective-permute-start.11 = (bf16[64,1536]{1,0:T(8,128)(2,1)S(1)}, bf16[64,1536]{1,0:T(8,128)(2,1)S(1)}, u32[]{:S(2)}, u32[]{:S(2)}) collective-permute-start(bf16[64,1536]{1,0:T(8,128)(2,1)S(1)} %collective-permute-done.7.p1), channel_id=1, source_target_pairs={{0,8},{1,9},{2,10},{3,11},{4,12},{5,13},{6,14},{7,15},{8,0},{9,1},... | collective-permute-start | bytes 589832 | tf_op jit(solution)/shard_map/ppermute | solution.py:32
  33.2 0.0 collective-permute-done.5.k2
  33.2 1.2 %collective-permute-start.4 = (bf16[128,512]{1,0:T(8,128)(2,1)S(1)}, bf16[128,512]{1,0:T(8,128)(2,1)S(1)}, u32[]{:S(2)}, u32[]{:S(2)}) collective-permute-start(bf16[128,512]{1,0:T(8,128)(2,1)S(1)} %get-tuple-element.13.k0), channel_id=1, source_target_pairs={{0,1},{1,0},{2,3},{3,2},{4,5},{5,4},{6,7},{7,6},{8,9},{9,8},{10,11... | collective-permute-start | bytes 393224 | tf_op jit(solution)/shard_map/ppermute | solution.py:32
  34.4 3.1 %load.1 = (bf16[1024,256]{1,0:T(8,128)(2,1)S(1)}, bf16[2048,256]{1,0:T(8,128)(2,1)S(1)}, bf16[1024,2048]{1,0:T(8,128)(2,1)S(1)}, bf16[1024,512]{1,0:T(8,128)(2,1)S(1)}, bf16[512,512]{1,0:T(8,128)(2,1)S(1)}) custom-call(bf16[16,1536]{1,0:T(8,128)(2,1)S(1)} %get-tuple-element.11.p0.after, bf16[1024,256]{1,0:T(8,128)(2,1)} %refs_0_.1, ...), custom_call_target="tpu_custom_call" | custom-call | bytes 14000000 | tf_op jit(solution)/shard_map/load/pallas_call | solution.py:114
  37.5 0.5 %collective-permute-done.4.k1 = bf16[128,512]{1,0:T(8,128)(2,1)S(1)} collective-permute-done((bf16[128,512]{1,0:T(8,128)(2,1)S(1)}, bf16[128,512]{1,0:T(8,128)(2,1)S(1)}, u32[]{:S(2)}, u32[]{:S(2)}) %collective-permute-start.4) | collective-permute-done | bytes 131104 | tf_op jit(solution)/shard_map/ppermute | solution.py:32
  38.0 0.6 %left_product.1.g = bf16[1024,512]{1,0:T(8,128)(2,1)S(1)} custom-call(bf16[128,512]{1,0:T(8,128)(2,1)S(1)} %get-tuple-element.13.k0, bf16[128,512]{1,0:T(8,128)(2,1)S(1)} %collective-permute-done.4.k1, bf16[128,512]{1,0:T(8,128)(2,1)S(1)} %collective-permute-done.5.k2, bf16[128,512]{1,0:T(8,128)(2,1)S(1)} %collective-permute-done.6.k3, ...), custom_call_target="tpu_custom_call" | custom-call | flops 270000000 | bytes 2000000 | tf_op jit(solution)/shard_map/left_product/pallas_call | solution.py:184
  38.6 0.0 collective-permute-done.10.p4
  38.6 0.0 collective-permute-done.13.p7
  38.6 0.0 collective-permute-done.12.p6
  38.6 0.0 collective-permute-done.11.p5
  38.6 4.3 %update.1 = (bf16[1024,2048]{1,0:T(8,128)(2,1)}, bf16[1024,512]{1,0:T(8,128)(2,1)}) custom-call(bf16[1024,512]{1,0:T(8,128)(2,1)S(1)} %left_product.1.g, bf16[64,1536]{1,0:T(8,128)(2,1)S(1)} %get-tuple-element.15.p0, bf16[64,1536]{1,0:T(8,128)(2,1)S(1)} %collective-permute-done.7.p1, bf16[64,1536]{1,0:T(8,128)(2,1)S(1)} %collective-permute-done.8.p2, ...), custom_call_target="tpu_custom_call" | custom-call | flops 3000000000 | bytes 16000000 | tf_op jit(solution)/shard_map/update/pallas_call | solution.py:226
  (1 shorter events, 0.0 us)
Async XLA Ops:
  3.0 16.6 %collective-permute-start.3 = (bf16[64,512]{1,0:T(8,128)(2,1)S(1)}, bf16[64,512]{1,0:T(8,128)(2,1)S(1)}, u32[]{:S(2)}, u32[]{:S(2)}) collective-permute-start(bf16[64,512]{1,0:T(8,128)(2,1)S(1)} %get-tuple-element.12.k0), channel_id=1, source_target_pairs={{0,4},{1,5},{2,6},{3,7},{4,0},{5,1},{6,2},{7,3},{8,12},{9,13},{10,... | collective-permute-start | bytes 196616 | tf_op jit(solution)/shard_map/ppermute | solution.py:32
  10.8 5.0 %collective-permute-start.2 = (bf16[16,1536]{1,0:T(8,128)(2,1)S(1)}, bf16[16,1536]{1,0:T(8,128)(2,1)S(1)}, u32[]{:S(2)}, u32[]{:S(2)}) collective-permute-start(bf16[16,1536]{1,0:T(8,128)(2,1)S(1)} %get-tuple-element.11.p0.after), channel_id=1, source_target_pairs={{0,192},{1,193},{2,194},{3,195},{4,196},{5,197},{6,198},{7,199},{8... | collective-permute-start | bytes 147464 | tf_op jit(solution)/shard_map/ppermute | solution.py:32
  12.4 7.1 %collective-permute-start.1 = (bf16[16,1536]{1,0:T(8,128)(2,1)S(1)}, bf16[16,1536]{1,0:T(8,128)(2,1)S(1)}, u32[]{:S(2)}, u32[]{:S(2)}) collective-permute-start(bf16[16,1536]{1,0:T(8,128)(2,1)S(1)} %get-tuple-element.11.p0.after), channel_id=1, source_target_pairs={{0,128},{1,129},{2,130},{3,131},{4,132},{5,133},{6,134},{7,135},{8... | collective-permute-start | bytes 147464 | tf_op jit(solution)/shard_map/ppermute | solution.py:32
  12.7 6.9 %collective-permute-start = (bf16[16,1536]{1,0:T(8,128)(2,1)S(1)}, bf16[16,1536]{1,0:T(8,128)(2,1)S(1)}, u32[]{:S(2)}, u32[]{:S(2)}) collective-permute-start(bf16[16,1536]{1,0:T(8,128)(2,1)S(1)} %get-tuple-element.11.p0.after), channel_id=1, source_target_pairs={{0,64},{1,65},{2,66},{3,67},{4,68},{5,69},{6,70},{7,71},{8,72},{9,... | collective-permute-start | bytes 147464 | tf_op jit(solution)/shard_map/ppermute | solution.py:32
  19.6 12.5 %collective-permute-start.9 = (bf16[64,1536]{1,0:T(8,128)(2,1)S(1)}, bf16[64,1536]{1,0:T(8,128)(2,1)S(1)}, u32[]{:S(2)}, u32[]{:S(2)}) collective-permute-start(bf16[64,1536]{1,0:T(8,128)(2,1)S(1)} %get-tuple-element.15.p0), channel_id=1, source_target_pairs={{0,48},{1,49},{2,50},{3,51},{4,52},{5,53},{6,54},{7,55},{8,56},{9,... | collective-permute-start | bytes 589832 | tf_op jit(solution)/shard_map/ppermute | solution.py:32
  22.4 10.1 %collective-permute-start.8 = (bf16[64,1536]{1,0:T(8,128)(2,1)S(1)}, bf16[64,1536]{1,0:T(8,128)(2,1)S(1)}, u32[]{:S(2)}, u32[]{:S(2)}) collective-permute-start(bf16[64,1536]{1,0:T(8,128)(2,1)S(1)} %get-tuple-element.15.p0), channel_id=1, source_target_pairs={{0,32},{1,33},{2,34},{3,35},{4,36},{5,37},{6,38},{7,39},{8,40},{9,... | collective-permute-start | bytes 589832 | tf_op jit(solution)/shard_map/ppermute | solution.py:32
  22.8 9.8 %collective-permute-start.7 = (bf16[64,1536]{1,0:T(8,128)(2,1)S(1)}, bf16[64,1536]{1,0:T(8,128)(2,1)S(1)}, u32[]{:S(2)}, u32[]{:S(2)}) collective-permute-start(bf16[64,1536]{1,0:T(8,128)(2,1)S(1)} %get-tuple-element.15.p0), channel_id=1, source_target_pairs={{0,16},{1,17},{2,18},{3,19},{4,20},{5,21},{6,22},{7,23},{8,24},{9,... | collective-permute-start | bytes 589832 | tf_op jit(solution)/shard_map/ppermute | solution.py:32
  23.1 7.9 %collective-permute-start.6 = (bf16[128,512]{1,0:T(8,128)(2,1)S(1)}, bf16[128,512]{1,0:T(8,128)(2,1)S(1)}, u32[]{:S(2)}, u32[]{:S(2)}) collective-permute-start(bf16[128,512]{1,0:T(8,128)(2,1)S(1)} %get-tuple-element.13.k0), channel_id=1, source_target_pairs={{0,3},{1,2},{2,1},{3,0},{4,7},{5,6},{6,5},{7,4},{8,11},{9,10},{10,... | collective-permute-start | bytes 393224 | tf_op jit(solution)/shard_map/ppermute | solution.py:32
  25.6 7.6 %collective-permute-start.5 = (bf16[128,512]{1,0:T(8,128)(2,1)S(1)}, bf16[128,512]{1,0:T(8,128)(2,1)S(1)}, u32[]{:S(2)}, u32[]{:S(2)}) collective-permute-start(bf16[128,512]{1,0:T(8,128)(2,1)S(1)} %get-tuple-element.13.k0), channel_id=1, source_target_pairs={{0,2},{1,3},{2,0},{3,1},{4,6},{5,7},{6,4},{7,5},{8,10},{9,11},{10,... | collective-permute-start | bytes 393224 | tf_op jit(solution)/shard_map/ppermute | solution.py:32
  30.9 7.6 %collective-permute-start.10 = (bf16[64,1536]{1,0:T(8,128)(2,1)S(1)}, bf16[64,1536]{1,0:T(8,128)(2,1)S(1)}, u32[]{:S(2)}, u32[]{:S(2)}) collective-permute-start(bf16[64,1536]{1,0:T(8,128)(2,1)S(1)} %get-tuple-element.15.p0), channel_id=1, source_target_pairs={{0,8},{1,9},{2,10},{3,11},{4,12},{5,13},{6,14},{7,15},{8,0},{9,1},... | collective-permute-start | bytes 589832 | tf_op jit(solution)/shard_map/ppermute | solution.py:32
  32.1 6.5 %collective-permute-start.13 = (bf16[64,1536]{1,0:T(8,128)(2,1)S(1)}, bf16[64,1536]{1,0:T(8,128)(2,1)S(1)}, u32[]{:S(2)}, u32[]{:S(2)}) collective-permute-start(bf16[64,1536]{1,0:T(8,128)(2,1)S(1)} %collective-permute-done.9.p3), channel_id=1, source_target_pairs={{0,8},{1,9},{2,10},{3,11},{4,12},{5,13},{6,14},{7,15},{8,0},{9,1},... | collective-permute-start | bytes 589832 | tf_op jit(solution)/shard_map/ppermute | solution.py:32
  32.5 6.1 %collective-permute-start.12 = (bf16[64,1536]{1,0:T(8,128)(2,1)S(1)}, bf16[64,1536]{1,0:T(8,128)(2,1)S(1)}, u32[]{:S(2)}, u32[]{:S(2)}) collective-permute-start(bf16[64,1536]{1,0:T(8,128)(2,1)S(1)} %collective-permute-done.8.p2), channel_id=1, source_target_pairs={{0,8},{1,9},{2,10},{3,11},{4,12},{5,13},{6,14},{7,15},{8,0},{9,1},... | collective-permute-start | bytes 589832 | tf_op jit(solution)/shard_map/ppermute | solution.py:32
  32.6 6.0 %collective-permute-start.11 = (bf16[64,1536]{1,0:T(8,128)(2,1)S(1)}, bf16[64,1536]{1,0:T(8,128)(2,1)S(1)}, u32[]{:S(2)}, u32[]{:S(2)}) collective-permute-start(bf16[64,1536]{1,0:T(8,128)(2,1)S(1)} %collective-permute-done.7.p1), channel_id=1, source_target_pairs={{0,8},{1,9},{2,10},{3,11},{4,12},{5,13},{6,14},{7,15},{8,0},{9,1},... | collective-permute-start | bytes 589832 | tf_op jit(solution)/shard_map/ppermute | solution.py:32
  33.2 4.8 %collective-permute-start.4 = (bf16[128,512]{1,0:T(8,128)(2,1)S(1)}, bf16[128,512]{1,0:T(8,128)(2,1)S(1)}, u32[]{:S(2)}, u32[]{:S(2)}) collective-permute-start(bf16[128,512]{1,0:T(8,128)(2,1)S(1)} %get-tuple-element.13.k0), channel_id=1, source_target_pairs={{0,1},{1,0},{2,3},{3,2},{4,5},{5,4},{6,7},{7,6},{8,9},{9,8},{10,11... | collective-permute-start | bytes 393224 | tf_op jit(solution)/shard_map/ppermute | solution.py:32

commit v2 on v1

v2 whole, which is shorter than its diff:
```python
import jax
import jax.numpy as jnp
from jax import lax
from jax.experimental import pallas as pl
from jax.experimental.pallas import tpu as pltpu
from jax.sharding import PartitionSpec as P


ROW, COL = 32, 8
BF = jnp.bfloat16
F32 = jnp.float32
VMEM = pl.BlockSpec(memory_space=pltpu.VMEM)
SMEM = pl.BlockSpec(memory_space=pltpu.SMEM)
ANY = pl.BlockSpec(memory_space=pl.ANY)
HBM = pl.BlockSpec(memory_space=pltpu.HBM)


def dot(a, b):
    return lax.dot_general(a, b, (((1,), (0,)), ((), ())), preferred_element_type=F32)


def dot_t(a, b):
    return lax.dot_general(a, b, (((1,), (1,)), ((), ())), preferred_element_type=F32)


def exchange(array, zl=0, y=0, core=0, zh=0, x=0):
    row_bits = zl * 8 + y * 2 + core
    col_bits = zh * 4 + x
    pairs = [
        (r * COL + c, (r ^ row_bits) * COL + (c ^ col_bits)) for r in range(ROW) for c in range(COL)
    ]
    return lax.ppermute(array, ("row", "col"), pairs)


def grant(mib):
    return pltpu.CompilerParams(vmem_limit_bytes=mib << 20)


def cost(flops, bytes_accessed):
    return pl.CostEstimate(flops=flops, bytes_accessed=bytes_accessed, transcendentals=0)


def in_hbm(array):
    return pltpu.with_memory_space_constraint(array, pltpu.HBM)


def start_all(sources, sems):
    copies = [pltpu.make_async_copy(a, b, sems.at[n]) for n, (a, b) in enumerate(sources)]
    for copy in copies:
        copy.start()
    return copies


def project_kernel(ranks_h, rows_h, left_h, bases_h, top_h, right_h, pivot_h,
                   pack, kt, bases, right, left, top, row_ranks, ranks, sems):
    tile = 512
    sources = [(top_h, top), (ranks_h, ranks), (rows_h, row_ranks)]
    for j in range(4):
        part = slice(j * tile, (j + 1) * tile)
        sources.append((right_h.at[part], right.at[part]))
    sources.append((left_h, left))
    for i in range(2):
        part = slice(i * tile, (i + 1) * tile)
        sources.append((bases_h.at[part], bases.at[part]))
    sources.append((pivot_h, pack.at[:, 1024:]))
    copies = start_all(sources, sems)
    lane = lax.broadcasted_iota(jnp.int32, (16, 256), 1)
    for copy in copies[:3]:
        copy.wait()
    for j in range(4):
        copies[3 + j].wait()
        part = dot(top[:, j * tile : (j + 1) * tile], right[j * tile : (j + 1) * tile, :])
        part = jnp.where(lane < ranks[j], part, 0.0)
        pack[:, j * 256 : (j + 1) * 256] = part.astype(BF)
    lane = lax.broadcasted_iota(jnp.int32, (64, 256), 1)
    copies[7].wait()
    for i in range(2):
        copies[8 + i].wait()
        part = dot(left[:, i * tile : (i + 1) * tile], bases[i * tile : (i + 1) * tile, :])
        part = jnp.where(lane < row_ranks[i], part, 0.0)
        kt[:, i * 256 : (i + 1) * 256] = part.astype(BF)
    copies[10].wait()


def project(ranks, row_ranks, left_t, bases, top, right, pivot):
    return pl.pallas_call(
        project_kernel,
        out_shape=(
            jax.ShapeDtypeStruct((16, 1536), BF),
            jax.ShapeDtypeStruct((64, 512), BF),
            jax.ShapeDtypeStruct((1024, 256), BF),
            jax.ShapeDtypeStruct((2048, 256), BF),
        ),
        in_specs=[HBM] * 7,
        out_specs=(VMEM,) * 4,
        scratch_shapes=[
            pltpu.VMEM((64, 1024), BF),
            pltpu.VMEM((16, 2048), BF),
            pltpu.SMEM((2,), jnp.int32),
            pltpu.SMEM((4,), jnp.int32),
            pltpu.SemaphoreType.DMA((11,)),
        ],
        compiler_params=grant(8),
        cost_estimate=cost(50_000_000, 1_800_000),
        name="project",
    )(*(in_hbm(a) for a in (ranks, row_ranks, left_t, bases, top, right, pivot)))


def load_kernel(*refs):
    count = (len(refs) - 1) // 2
    copies = start_all(list(zip(refs[:count], refs[count:-1])), refs[-1])
    for copy in copies:
        copy.wait()


def load(*arrays):
    return pl.pallas_call(
        load_kernel,
        out_shape=[jax.ShapeDtypeStruct(a.shape, a.dtype) for a in arrays],
        in_specs=[HBM] * len(arrays),
        out_specs=[VMEM] * len(arrays),
        scratch_shapes=[pltpu.SemaphoreType.DMA((len(arrays),))],
        compiler_params=grant(10),
        cost_estimate=cost(0, 8_000_000),
    )(*(in_hbm(a) for a in arrays))


def join_kernel(*refs):
    out = refs[-1]
    rows = refs[0].shape[0]
    for n, piece in enumerate(refs[:-1]):
        out[n * rows : (n + 1) * rows, :] = piece[...]


def join(pieces):
    rows, columns = pieces[0].shape
    return pl.pallas_call(
        join_kernel,
        out_shape=jax.ShapeDtypeStruct((len(pieces) * rows, columns), BF),
        in_specs=[VMEM] * len(pieces),
        out_specs=VMEM,
        compiler_params=grant(4),
        cost_estimate=cost(0, 300_000),
    )(*pieces)


def place():
    r = lax.axis_index("row")
    c = lax.axis_index("col")
    return r // 8, (r // 2) % 4, r % 2, c // 4, c % 4


def blocks():
    zl, y, core, zh, x = place()
    n = 0
    for half in range(2):
        for dy in range(4):
            for dz in range(4):
                z_from, y_from, core_from = zl ^ dz, y ^ dy, core ^ half
                natural = (z_from * 4 + y_from) * 32 + core_from * 16
                col_from = z_from * 2 + y_from // 2
                stacked = (
                    ((col_from % 4) ^ x) * 128
                    + ((col_from // 4) ^ zh) * 64
                    + (y_from % 2) * 32
                    + core_from * 16
                )
                yield n * 16, pl.multiple_of(natural, 16), pl.multiple_of(stacked, 16)
                n += 1


def left_kernel(k0, k1, k2, k3, bases, g_ref, stack, ordered):
    for n, piece in enumerate((k0, k1, k2, k3)):
        stack[n * 128 : (n + 1) * 128, :] = piece[...]
    for at, _, stacked in blocks():
        ordered[at : at + 16, :] = stack[pl.ds(stacked, 16), :]
    for i in range(2):
        rows = slice(i * 512, (i + 1) * 512)
        g_ref[rows, :] = dot_t(bases[rows, :], ordered[:, i * 256 : (i + 1) * 256]).astype(BF)


def left_product(parts, bases):
    return pl.pallas_call(
        left_kernel,
        out_shape=jax.ShapeDtypeStruct((1024, 512), BF),
        in_specs=[VMEM] * 5,
        out_specs=VMEM,
        scratch_shapes=[pltpu.VMEM((512, 512), BF), pltpu.VMEM((512, 512), BF)],
        cost_estimate=cost(270_000_000, 2_000_000),
        compiler_params=grant(10),
        name="left_product",
    )(*parts, bases)


def solve_kernel(p0, p1, p2, p3, p4, p5, p6, p7, inverse, ordered, natural, solved):
    pieces = (p0, p1, p2, p3, p4, p5, p6, p7)
    for at, to, _ in blocks():
        natural[pl.ds(to, 16), :] = pieces[at // 64][at % 64 : at % 64 + 16, 1024:]
    solved[...] = dot(inverse[...], natural[...]).astype(BF)
    for at, to, _ in blocks():
        ordered[at : at + 16, :] = solved[pl.ds(to, 16), :]


def solve(pieces, inverse):
    return pl.pallas_call(
        solve_kernel,
        out_shape=jax.ShapeDtypeStruct((512, 512), BF),
        in_specs=[VMEM] * 9,
        out_specs=VMEM,
        scratch_shapes=[pltpu.VMEM((512, 512), BF), pltpu.VMEM((512, 512), BF)],
        compiler_params=grant(6),
        cost_estimate=cost(270_000_000, 2_000_000),
        name="solve",
    )(*pieces, inverse)


def update_kernel(g, p0, p1, p2, p3, p4, p5, p6, p7, right, y, slab, rhs,
                  slab_out, rhs_out, wide, slab_v, rhs_v, sems):
    pieces = (p0, p1, p2, p3, p4, p5, p6, p7)
    tile = 512
    for j in range(4):
        core = jnp.concatenate([p[:, j * 256 : (j + 1) * 256] for p in pieces], axis=0)
        for i in range(2):
            rows = slice(i * tile, (i + 1) * tile)
            wide[j, rows, :] = dot(g[rows, :], core).astype(BF)
    stores = []
    for j in range(4):
        cols = slice(j * tile, (j + 1) * tile)
        change = dot_t(wide[j], right[cols, :])
        slab_v[:, cols] = (slab[:, cols].astype(F32) - change).astype(BF)
        stores.append(pltpu.make_async_copy(slab_v.at[:, cols], slab_out.at[:, cols], sems.at[j]))
        stores[-1].start()
    rhs_v[...] = (rhs[...].astype(F32) - dot(g[...], y[...])).astype(BF)
    stores.append(pltpu.make_async_copy(rhs_v, rhs_out, sems.at[4]))
    stores[-1].start()
    for copy in stores:
        copy.wait()


def update(g, pieces, right, y, slab, rhs):
    return pl.pallas_call(
        update_kernel,
        out_shape=(
            jax.ShapeDtypeStruct((1024, 2048), BF),
            jax.ShapeDtypeStruct((1024, 512), BF),
        ),
        in_specs=[VMEM] * 13,
        out_specs=(HBM, HBM),
        scratch_shapes=[
            pltpu.VMEM((4, 1024, 256), BF),
            pltpu.VMEM((1024, 2048), BF),
            pltpu.VMEM((1024, 512), BF),
            pltpu.SemaphoreType.DMA((5,)),
        ],
        compiler_params=grant(24),
        cost_estimate=cost(2_700_000_000, 12_000_000),
        name="update",
    )(g, *pieces, right, y, slab, rhs)


def per_device(
    slab,
    panel_left,
    panel_top,
    row_bases,
    col_bases,
    row_ranks,
    col_ranks,
    pivot_inverse,
    pivot_rhs,
    rhs,
):
    pack, part, bases, right = project(
        col_ranks, row_ranks, panel_left.T, row_bases, panel_top, col_bases, pivot_rhs
    )
    (inverse,) = load(pivot_inverse)
    packs = [pack] + [exchange(pack, zl=d) for d in (1, 2, 3)]
    part_far = exchange(part, zh=1)
    piece = join(packs)
    pieces = [piece] + [exchange(piece, y=d) for d in (1, 2, 3)]
    left_part = join((part, part_far))
    lefts = [left_part] + [exchange(left_part, x=d) for d in (1, 2, 3)]
    twins = [exchange(p, core=1) for p in pieces]
    y = solve(pieces + twins, inverse)
    g = left_product(lefts, bases)
    return update(g, pieces + twins, right, y, slab, rhs)


def solution(mesh):
    in_specs = (
        P("row", "col"),
        P("row", "col"),
        P("row", "col"),
        P("row", None),
        P("col", None),
        P("row"),
        P("col"),
        P(),
        P("row", "col"),
        P("row", "col"),
    )
    out_specs = (P("row", "col"), P("row", "col"))
    return jax.shard_map(
        per_device, mesh=mesh, in_specs=in_specs, out_specs=out_specs, check_vma=False
    )
```

time: 43.1 us -> 38.8 us (0.900)
  the two profiles are of different devices: /device:TPU:1 before, /device:TPU:62 now
where the time goes in v2:
time: 38.8 us; the launch traced here: 38.7 us
  starting transfers between devices  18 us (46%)
  waiting for transfers between devices  11.3 us (29%)
  Pallas kernels  8.54 us (22%)
  between operations  0.75 us (2%)
    ppermute x14, starting transfers between devices, exchange(): return lax.ppermute(array, ('row', 'col'), pairs)  18 us
    ppermute x14, waiting for transfers between devices, exchange(): return lax.ppermute(array, ('row', 'col'), pairs)  11.3 us
    pallas_call x1, Pallas kernels, update(): pl.pallas_call(update_kernel, out_shape=(jax.ShapeDtypeStruct((1024, 2048...  3.93 us
    pallas_call x1, Pallas kernels, project(): pl.pallas_call(project_kernel, out_shape=(jax.ShapeDtypeStruct((16, 1536)...  2.38 us
    pallas_call x1, Pallas kernels, load(): pl.pallas_call(load_kernel, out_shape=[jax.ShapeDtypeStruct(a.shape, a.dt...  1.05 us
  transfers between devices with their start and end apart: 14, of which 3 were waited for; matrix products, arithmetic and copies ran while one was open for 0% of the time, Pallas kernels for 4%

profile of v2, /device:TPU:62, one launch (start us, length us, event | category | flops | bytes accessed | tf_op | source)
XLA Modules:
  0.0 38.7 jit_solution(8708496657857170270)
XLA Ops:
  0.6 0.0 copy-start.1
  0.6 0.0 copy-start
  0.7 2.4 %project.1 = (bf16[16,1536]{1,0:T(8,128)(2,1)S(1)}, bf16[64,512]{1,0:T(8,128)(2,1)S(1)}, bf16[1024,256]{1,0:T(8,128)(2,1)S(1)}, bf16[2048,256]{1,0:T(8,128)(2,1)S(1)}) custom-call(s32[4]{0:T(128)} %ranks_h.1, s32[2]{0:T(128)} %rows_h.1, bf16[64,1024]{1,0:T(8,128)(2,1)} %bitcast.1, bf16[1024,256]{1,0:T(8,128)(2,1)} %bases_h.1, bf16[16,2048]{1,0:T(8,128)(2,1)} %top_h.1, ...), custom_call_target="tpu_custom_call" | custom-call | flops 50000000 | bytes 1800000 | tf_op jit(solution)/shard_map/project/pallas_call | solution.py:86
  3.0 2.0 %collective-permute-start.6 = (bf16[16,1536]{1,0:T(8,128)(2,1)S(1)}, bf16[16,1536]{1,0:T(8,128)(2,1)S(1)}, u32[]{:S(2)}, u32[]{:S(2)}) collective-permute-start(bf16[16,1536]{1,0:T(8,128)(2,1)S(1)} %get-tuple-element.8.refs_0_), channel_id=1, source_target_pairs={{0,192},{1,193},{2,194},{3,195},{4,196},{5,197},{6,198},{7,199},{8... | collective-permute-start | bytes 147464 | tf_op jit(solution)/shard_map/ppermute | solution.py:32
  5.0 1.5 %collective-permute-start.5 = (bf16[16,1536]{1,0:T(8,128)(2,1)S(1)}, bf16[16,1536]{1,0:T(8,128)(2,1)S(1)}, u32[]{:S(2)}, u32[]{:S(2)}) collective-permute-start(bf16[16,1536]{1,0:T(8,128)(2,1)S(1)} %get-tuple-element.8.refs_0_), channel_id=1, source_target_pairs={{0,128},{1,129},{2,130},{3,131},{4,132},{5,133},{6,134},{7,135},{8... | collective-permute-start | bytes 147464 | tf_op jit(solution)/shard_map/ppermute | solution.py:32
  6.5 1.4 %collective-permute-start.4 = (bf16[16,1536]{1,0:T(8,128)(2,1)S(1)}, bf16[16,1536]{1,0:T(8,128)(2,1)S(1)}, u32[]{:S(2)}, u32[]{:S(2)}) collective-permute-start(bf16[16,1536]{1,0:T(8,128)(2,1)S(1)} %get-tuple-element.8.refs_0_), channel_id=1, source_target_pairs={{0,64},{1,65},{2,66},{3,67},{4,68},{5,69},{6,70},{7,71},{8,72},{9,... | collective-permute-start | bytes 147464 | tf_op jit(solution)/shard_map/ppermute | solution.py:32
  7.9 5.0 %collective-permute-start = (bf16[64,512]{1,0:T(8,128)(2,1)S(1)}, bf16[64,512]{1,0:T(8,128)(2,1)S(1)}, u32[]{:S(2)}, u32[]{:S(2)}) collective-permute-start(bf16[64,512]{1,0:T(8,128)(2,1)S(1)} %get-tuple-element.6.refs_0_), channel_id=1, source_target_pairs={{0,4},{1,5},{2,6},{3,7},{4,0},{5,1},{6,2},{7,3},{8,12},{9,13},{10,... | collective-permute-start | bytes 196616 | tf_op jit(solution)/shard_map/ppermute | solution.py:32
  12.9 0.0 collective-permute-done.6.refs_3_
  12.9 0.0 collective-permute-done.5.refs_2_
  12.9 0.0 collective-permute-done.4.refs_1_
  12.9 0.3 collective-permute-start.9
  13.3 2.6 %collective-permute-start.8 = (bf16[64,1536]{1,0:T(8,128)(2,1)S(1)}, bf16[64,1536]{1,0:T(8,128)(2,1)S(1)}, u32[]{:S(2)}, u32[]{:S(2)}) collective-permute-start(bf16[64,1536]{1,0:T(8,128)(2,1)S(1)} %shard_map.114.p0), channel_id=1, source_target_pairs={{0,32},{1,33},{2,34},{3,35},{4,36},{5,37},{6,38},{7,39},{8,40},{9,... | collective-permute-start | bytes 589832 | tf_op jit(solution)/shard_map/ppermute | solution.py:32
  15.8 1.3 %collective-permute-start.7 = (bf16[64,1536]{1,0:T(8,128)(2,1)S(1)}, bf16[64,1536]{1,0:T(8,128)(2,1)S(1)}, u32[]{:S(2)}, u32[]{:S(2)}) collective-permute-start(bf16[64,1536]{1,0:T(8,128)(2,1)S(1)} %shard_map.114.p0), channel_id=1, source_target_pairs={{0,16},{1,17},{2,18},{3,19},{4,20},{5,21},{6,22},{7,23},{8,24},{9,... | collective-permute-start | bytes 589832 | tf_op jit(solution)/shard_map/ppermute | solution.py:32
  17.1 1.3 %collective-permute-done.refs_1_ = bf16[64,512]{1,0:T(8,128)(2,1)S(1)} collective-permute-done((bf16[64,512]{1,0:T(8,128)(2,1)S(1)}, bf16[64,512]{1,0:T(8,128)(2,1)S(1)}, u32[]{:S(2)}, u32[]{:S(2)}) %collective-permute-start) | collective-permute-done | bytes 65568 | tf_op jit(solution)/shard_map/ppermute | solution.py:32
  18.4 0.6 %collective-permute-start.3 = (bf16[128,512]{1,0:T(8,128)(2,1)S(1)}, bf16[128,512]{1,0:T(8,128)(2,1)S(1)}, u32[]{:S(2)}, u32[]{:S(2)}) collective-permute-start(bf16[128,512]{1,0:T(8,128)(2,1)S(1)} %shard_map.113.k0), channel_id=1, source_target_pairs={{0,3},{1,2},{2,1},{3,0},{4,7},{5,6},{6,5},{7,4},{8,11},{9,10},{10,... | collective-permute-start | bytes 393224 | tf_op jit(solution)/shard_map/ppermute | solution.py:32
  19.0 2.4 %collective-permute-start.2 = (bf16[128,512]{1,0:T(8,128)(2,1)S(1)}, bf16[128,512]{1,0:T(8,128)(2,1)S(1)}, u32[]{:S(2)}, u32[]{:S(2)}) collective-permute-start(bf16[128,512]{1,0:T(8,128)(2,1)S(1)} %shard_map.113.k0), channel_id=1, source_target_pairs={{0,2},{1,3},{2,0},{3,1},{4,6},{5,7},{6,4},{7,5},{8,10},{9,11},{10,... | collective-permute-start | bytes 393224 | tf_op jit(solution)/shard_map/ppermute | solution.py:32
  21.4 5.6 %collective-permute-done.3.k3 = bf16[128,512]{1,0:T(8,128)(2,1)S(1)} collective-permute-done((bf16[128,512]{1,0:T(8,128)(2,1)S(1)}, bf16[128,512]{1,0:T(8,128)(2,1)S(1)}, u32[]{:S(2)}, u32[]{:S(2)}) %collective-permute-start.3) | collective-permute-done | bytes 131104 | tf_op jit(solution)/shard_map/ppermute | solution.py:32
  27.0 0.0 collective-permute-start.10
  27.0 0.0 collective-permute-done.9.p3
  27.0 0.5 %collective-permute-start.13 = (bf16[64,1536]{1,0:T(8,128)(2,1)S(1)}, bf16[64,1536]{1,0:T(8,128)(2,1)S(1)}, u32[]{:S(2)}, u32[]{:S(2)}) collective-permute-start(bf16[64,1536]{1,0:T(8,128)(2,1)S(1)} %collective-permute-done.9.p3), channel_id=1, source_target_pairs={{0,8},{1,9},{2,10},{3,11},{4,12},{5,13},{6,14},{7,15},{8,0},{9,1},... | collective-permute-start | bytes 589832 | tf_op jit(solution)/shard_map/ppermute | solution.py:32
  27.5 0.0 collective-permute-done.8.p2
  27.5 0.1 collective-permute-start.12
  27.6 0.0 collective-permute-done.7.p1
  27.6 0.4 %collective-permute-start.11 = (bf16[64,1536]{1,0:T(8,128)(2,1)S(1)}, bf16[64,1536]{1,0:T(8,128)(2,1)S(1)}, u32[]{:S(2)}, u32[]{:S(2)}) collective-permute-start(bf16[64,1536]{1,0:T(8,128)(2,1)S(1)} %collective-permute-done.7.p1), channel_id=1, source_target_pairs={{0,8},{1,9},{2,10},{3,11},{4,12},{5,13},{6,14},{7,15},{8,0},{9,1},... | collective-permute-start | bytes 589832 | tf_op jit(solution)/shard_map/ppermute | solution.py:32
  28.0 0.0 collective-permute-done.2.k2
  28.0 0.0 collective-permute-start.1
  28.0 1.1 %shard_map.115.inverse = bf16[512,512]{1,0:T(8,128)(2,1)S(1)} custom-call(bf16[512,512]{1,0:T(8,128)(2,1)} %refs_0_.1), custom_call_target="tpu_custom_call" | custom-call | bytes 8000000 | tf_op jit(solution)/shard_map/pallas_call | solution.py:117
  29.1 4.4 %collective-permute-done.1.k1 = bf16[128,512]{1,0:T(8,128)(2,1)S(1)} collective-permute-done((bf16[128,512]{1,0:T(8,128)(2,1)S(1)}, bf16[128,512]{1,0:T(8,128)(2,1)S(1)}, u32[]{:S(2)}, u32[]{:S(2)}) %collective-permute-start.1) | collective-permute-done | bytes 131104 | tf_op jit(solution)/shard_map/ppermute | solution.py:32
  33.5 0.6 %left_product.1.g = bf16[1024,512]{1,0:T(8,128)(2,1)S(1)} custom-call(bf16[128,512]{1,0:T(8,128)(2,1)S(1)} %shard_map.113.k0, bf16[128,512]{1,0:T(8,128)(2,1)S(1)} %collective-permute-done.1.k1, bf16[128,512]{1,0:T(8,128)(2,1)S(1)} %collective-permute-done.2.k2, bf16[128,512]{1,0:T(8,128)(2,1)S(1)} %collective-permute-done.3.k3, ...), custom_call_target="tpu_custom_call" | custom-call | flops 270000000 | bytes 2000000 | tf_op jit(solution)/shard_map/left_product/pallas_call | solution.py:183
  34.1 0.0 collective-permute-done.10.p4
  34.1 0.0 collective-permute-done.13.p7
  34.1 0.0 collective-permute-done.12.p6
  34.2 0.0 collective-permute-done.11.p5
  34.2 0.6 %solve.1.y = bf16[512,512]{1,0:T(8,128)(2,1)S(1)} custom-call(bf16[64,1536]{1,0:T(8,128)(2,1)S(1)} %shard_map.114.p0, bf16[64,1536]{1,0:T(8,128)(2,1)S(1)} %collective-permute-done.7.p1, bf16[64,1536]{1,0:T(8,128)(2,1)S(1)} %collective-permute-done.8.p2, bf16[64,1536]{1,0:T(8,128)(2,1)S(1)} %collective-permute-done.9.p3, ...), custom_call_target="tpu_custom_call" | custom-call | flops 270000000 | bytes 2000000 | tf_op jit(solution)/shard_map/solve/pallas_call | solution.py:205
  34.7 0.0 copy-done.1
  34.7 0.0 copy-done
  34.7 3.9 %update.1 = (bf16[1024,2048]{1,0:T(8,128)(2,1)}, bf16[1024,512]{1,0:T(8,128)(2,1)}) custom-call(bf16[1024,512]{1,0:T(8,128)(2,1)S(1)} %left_product.1.g, bf16[64,1536]{1,0:T(8,128)(2,1)S(1)} %shard_map.114.p0, bf16[64,1536]{1,0:T(8,128)(2,1)S(1)} %collective-permute-done.7.p1, bf16[64,1536]{1,0:T(8,128)(2,1)S(1)} %collective-permute-done.8.p2, ...), custom_call_target="tpu_custom_call" | custom-call | flops 2700000000 | bytes 12000000 | tf_op jit(solution)/shard_map/update/pallas_call | solution.py:241
  (2 shorter events, 0.0 us)
Async XLA Ops:
  0.6 34.1 %copy-start.1 = (bf16[1024,512]{1,0:T(8,128)(2,1)S(1)}, bf16[1024,512]{1,0:T(8,128)(2,1)}, u32[]{:S(2)}) copy-start(bf16[1024,512]{1,0:T(8,128)(2,1)} %rhs.1) | copy-start | bytes 3145732
  0.6 34.1 %copy-start = (bf16[1024,2048]{1,0:T(8,128)(2,1)S(1)}, bf16[1024,2048]{1,0:T(8,128)(2,1)}, u32[]{:S(2)}) copy-start(bf16[1024,2048]{1,0:T(8,128)(2,1)} %slab.1) | copy-start | bytes 12582916
  3.0 9.9 %collective-permute-start.6 = (bf16[16,1536]{1,0:T(8,128)(2,1)S(1)}, bf16[16,1536]{1,0:T(8,128)(2,1)S(1)}, u32[]{:S(2)}, u32[]{:S(2)}) collective-permute-start(bf16[16,1536]{1,0:T(8,128)(2,1)S(1)} %get-tuple-element.8.refs_0_), channel_id=1, source_target_pairs={{0,192},{1,193},{2,194},{3,195},{4,196},{5,197},{6,198},{7,199},{8... | collective-permute-start | bytes 147464 | tf_op jit(solution)/shard_map/ppermute | solution.py:32
  5.0 7.9 %collective-permute-start.5 = (bf16[16,1536]{1,0:T(8,128)(2,1)S(1)}, bf16[16,1536]{1,0:T(8,128)(2,1)S(1)}, u32[]{:S(2)}, u32[]{:S(2)}) collective-permute-start(bf16[16,1536]{1,0:T(8,128)(2,1)S(1)} %get-tuple-element.8.refs_0_), channel_id=1, source_target_pairs={{0,128},{1,129},{2,130},{3,131},{4,132},{5,133},{6,134},{7,135},{8... | collective-permute-start | bytes 147464 | tf_op jit(solution)/shard_map/ppermute | solution.py:32
  6.5 6.4 %collective-permute-start.4 = (bf16[16,1536]{1,0:T(8,128)(2,1)S(1)}, bf16[16,1536]{1,0:T(8,128)(2,1)S(1)}, u32[]{:S(2)}, u32[]{:S(2)}) collective-permute-start(bf16[16,1536]{1,0:T(8,128)(2,1)S(1)} %get-tuple-element.8.refs_0_), channel_id=1, source_target_pairs={{0,64},{1,65},{2,66},{3,67},{4,68},{5,69},{6,70},{7,71},{8,72},{9,... | collective-permute-start | bytes 147464 | tf_op jit(solution)/shard_map/ppermute | solution.py:32
  7.9 10.5 %collective-permute-start = (bf16[64,512]{1,0:T(8,128)(2,1)S(1)}, bf16[64,512]{1,0:T(8,128)(2,1)S(1)}, u32[]{:S(2)}, u32[]{:S(2)}) collective-permute-start(bf16[64,512]{1,0:T(8,128)(2,1)S(1)} %get-tuple-element.6.refs_0_), channel_id=1, source_target_pairs={{0,4},{1,5},{2,6},{3,7},{4,0},{5,1},{6,2},{7,3},{8,12},{9,13},{10,... | collective-permute-start | bytes 196616 | tf_op jit(solution)/shard_map/ppermute | solution.py:32
  12.9 14.0 %collective-permute-start.9 = (bf16[64,1536]{1,0:T(8,128)(2,1)S(1)}, bf16[64,1536]{1,0:T(8,128)(2,1)S(1)}, u32[]{:S(2)}, u32[]{:S(2)}) collective-permute-start(bf16[64,1536]{1,0:T(8,128)(2,1)S(1)} %shard_map.114.p0), channel_id=1, source_target_pairs={{0,48},{1,49},{2,50},{3,51},{4,52},{5,53},{6,54},{7,55},{8,56},{9,... | collective-permute-start | bytes 589832 | tf_op jit(solution)/shard_map/ppermute | solution.py:32
  13.3 14.2 %collective-permute-start.8 = (bf16[64,1536]{1,0:T(8,128)(2,1)S(1)}, bf16[64,1536]{1,0:T(8,128)(2,1)S(1)}, u32[]{:S(2)}, u32[]{:S(2)}) collective-permute-start(bf16[64,1536]{1,0:T(8,128)(2,1)S(1)} %shard_map.114.p0), channel_id=1, source_target_pairs={{0,32},{1,33},{2,34},{3,35},{4,36},{5,37},{6,38},{7,39},{8,40},{9,... | collective-permute-start | bytes 589832 | tf_op jit(solution)/shard_map/ppermute | solution.py:32
  15.8 11.8 %collective-permute-start.7 = (bf16[64,1536]{1,0:T(8,128)(2,1)S(1)}, bf16[64,1536]{1,0:T(8,128)(2,1)S(1)}, u32[]{:S(2)}, u32[]{:S(2)}) collective-permute-start(bf16[64,1536]{1,0:T(8,128)(2,1)S(1)} %shard_map.114.p0), channel_id=1, source_target_pairs={{0,16},{1,17},{2,18},{3,19},{4,20},{5,21},{6,22},{7,23},{8,24},{9,... | collective-permute-start | bytes 589832 | tf_op jit(solution)/shard_map/ppermute | solution.py:32
  18.4 8.6 %collective-permute-start.3 = (bf16[128,512]{1,0:T(8,128)(2,1)S(1)}, bf16[128,512]{1,0:T(8,128)(2,1)S(1)}, u32[]{:S(2)}, u32[]{:S(2)}) collective-permute-start(bf16[128,512]{1,0:T(8,128)(2,1)S(1)} %shard_map.113.k0), channel_id=1, source_target_pairs={{0,3},{1,2},{2,1},{3,0},{4,7},{5,6},{6,5},{7,4},{8,11},{9,10},{10,... | collective-permute-start | bytes 393224 | tf_op jit(solution)/shard_map/ppermute | solution.py:32
  19.0 9.0 %collective-permute-start.2 = (bf16[128,512]{1,0:T(8,128)(2,1)S(1)}, bf16[128,512]{1,0:T(8,128)(2,1)S(1)}, u32[]{:S(2)}, u32[]{:S(2)}) collective-permute-start(bf16[128,512]{1,0:T(8,128)(2,1)S(1)} %shard_map.113.k0), channel_id=1, source_target_pairs={{0,2},{1,3},{2,0},{3,1},{4,6},{5,7},{6,4},{7,5},{8,10},{9,11},{10,... | collective-permute-start | bytes 393224 | tf_op jit(solution)/shard_map/ppermute | solution.py:32
  27.0 7.1 %collective-permute-start.10 = (bf16[64,1536]{1,0:T(8,128)(2,1)S(1)}, bf16[64,1536]{1,0:T(8,128)(2,1)S(1)}, u32[]{:S(2)}, u32[]{:S(2)}) collective-permute-start(bf16[64,1536]{1,0:T(8,128)(2,1)S(1)} %shard_map.114.p0), channel_id=1, source_target_pairs={{0,8},{1,9},{2,10},{3,11},{4,12},{5,13},{6,14},{7,15},{8,0},{9,1},... | collective-permute-start | bytes 589832 | tf_op jit(solution)/shard_map/ppermute | solution.py:32
  27.0 7.1 %collective-permute-start.13 = (bf16[64,1536]{1,0:T(8,128)(2,1)S(1)}, bf16[64,1536]{1,0:T(8,128)(2,1)S(1)}, u32[]{:S(2)}, u32[]{:S(2)}) collective-permute-start(bf16[64,1536]{1,0:T(8,128)(2,1)S(1)} %collective-permute-done.9.p3), channel_id=1, source_target_pairs={{0,8},{1,9},{2,10},{3,11},{4,12},{5,13},{6,14},{7,15},{8,0},{9,1},... | collective-permute-start | bytes 589832 | tf_op jit(solution)/shard_map/ppermute | solution.py:32
  27.5 6.6 %collective-permute-start.12 = (bf16[64,1536]{1,0:T(8,128)(2,1)S(1)}, bf16[64,1536]{1,0:T(8,128)(2,1)S(1)}, u32[]{:S(2)}, u32[]{:S(2)}) collective-permute-start(bf16[64,1536]{1,0:T(8,128)(2,1)S(1)} %collective-permute-done.8.p2), channel_id=1, source_target_pairs={{0,8},{1,9},{2,10},{3,11},{4,12},{5,13},{6,14},{7,15},{8,0},{9,1},... | collective-permute-start | bytes 589832 | tf_op jit(solution)/shard_map/ppermute | solution.py:32
  27.6 6.6 %collective-permute-start.11 = (bf16[64,1536]{1,0:T(8,128)(2,1)S(1)}, bf16[64,1536]{1,0:T(8,128)(2,1)S(1)}, u32[]{:S(2)}, u32[]{:S(2)}) collective-permute-start(bf16[64,1536]{1,0:T(8,128)(2,1)S(1)} %collective-permute-done.7.p1), channel_id=1, source_target_pairs={{0,8},{1,9},{2,10},{3,11},{4,12},{5,13},{6,14},{7,15},{8,0},{9,1},... | collective-permute-start | bytes 589832 | tf_op jit(solution)/shard_map/ppermute | solution.py:32
  28.0 5.5 %collective-permute-start.1 = (bf16[128,512]{1,0:T(8,128)(2,1)S(1)}, bf16[128,512]{1,0:T(8,128)(2,1)S(1)}, u32[]{:S(2)}, u32[]{:S(2)}) collective-permute-start(bf16[128,512]{1,0:T(8,128)(2,1)S(1)} %shard_map.113.k0), channel_id=1, source_target_pairs={{0,1},{1,0},{2,3},{3,2},{4,5},{5,4},{6,7},{7,6},{8,9},{9,8},{10,11... | collective-permute-start | bytes 393224 | tf_op jit(solution)/shard_map/ppermute | solution.py:32

commit v3 on v2

--- a/solution.py
+++ b/solution.py
@@ -63,23 +63,18 @@
         part = slice(i * tile, (i + 1) * tile)
         sources.append((bases_h.at[part], bases.at[part]))
     sources.append((pivot_h, pack.at[:, 1024:]))
-    copies = start_all(sources, sems)
+    for copy in start_all(sources, sems):
+        copy.wait()
     lane = lax.broadcasted_iota(jnp.int32, (16, 256), 1)
-    for copy in copies[:3]:
-        copy.wait()
-    for j in range(4):
-        copies[3 + j].wait()
+    for j in range(4):
         part = dot(top[:, j * tile : (j + 1) * tile], right[j * tile : (j + 1) * tile, :])
         part = jnp.where(lane < ranks[j], part, 0.0)
         pack[:, j * 256 : (j + 1) * 256] = part.astype(BF)
     lane = lax.broadcasted_iota(jnp.int32, (64, 256), 1)
-    copies[7].wait()
     for i in range(2):
-        copies[8 + i].wait()
         part = dot(left[:, i * tile : (i + 1) * tile], bases[i * tile : (i + 1) * tile, :])
         part = jnp.where(lane < row_ranks[i], part, 0.0)
         kt[:, i * 256 : (i + 1) * 256] = part.astype(BF)
-    copies[10].wait()
 
 
 def project(ranks, row_ranks, left_t, bases, top, right, pivot):
@@ -159,8 +154,9 @@
                 z_from, y_from, core_from = zl ^ dz, y ^ dy, core ^ half
                 natural = (z_from * 4 + y_from) * 32 + core_from * 16
                 col_from = z_from * 2 + y_from // 2
+                turn = (col_from % 4) ^ x
                 stacked = (
-                    ((col_from % 4) ^ x) * 128
+                    ((turn // 2) ^ ((turn % 2) * 3)) * 128
                     + ((col_from // 4) ^ zh) * 64
                     + (y_from % 2) * 32
                     + core_from * 16
@@ -169,60 +165,44 @@
                 n += 1
 
 
-def left_kernel(k0, k1, k2, k3, bases, g_ref, stack, ordered):
-    for n, piece in enumerate((k0, k1, k2, k3)):
-        stack[n * 128 : (n + 1) * 128, :] = piece[...]
-    for at, _, stacked in blocks():
-        ordered[at : at + 16, :] = stack[pl.ds(stacked, 16), :]
-    for i in range(2):
-        rows = slice(i * 512, (i + 1) * 512)
-        g_ref[rows, :] = dot_t(bases[rows, :], ordered[:, i * 256 : (i + 1) * 256]).astype(BF)
-
-
-def left_product(parts, bases):
-    return pl.pallas_call(
-        left_kernel,
-        out_shape=jax.ShapeDtypeStruct((1024, 512), BF),
-        in_specs=[VMEM] * 5,
-        out_specs=VMEM,
-        scratch_shapes=[pltpu.VMEM((512, 512), BF), pltpu.VMEM((512, 512), BF)],
-        cost_estimate=cost(270_000_000, 2_000_000),
-        compiler_params=grant(10),
-        name="left_product",
-    )(*parts, bases)
-
-
-def solve_kernel(p0, p1, p2, p3, p4, p5, p6, p7, inverse, ordered, natural, solved):
+def solve_kernel(p0, p1, p2, p3, p4, p5, p6, p7, inverse, middle, ordered, natural, solved):
     pieces = (p0, p1, p2, p3, p4, p5, p6, p7)
     for at, to, _ in blocks():
         natural[pl.ds(to, 16), :] = pieces[at // 64][at % 64 : at % 64 + 16, 1024:]
     solved[...] = dot(inverse[...], natural[...]).astype(BF)
-    for at, to, _ in blocks():
-        ordered[at : at + 16, :] = solved[pl.ds(to, 16), :]
+    for at, to, stacked in blocks():
+        middle[pl.ds(stacked, 16), :] = pieces[at // 64][at % 64 : at % 64 + 16, :1024]
+    for _, to, stacked in blocks():
+        ordered[pl.ds(stacked, 16), :] = solved[pl.ds(to, 16), :]
 
 
 def solve(pieces, inverse):
     return pl.pallas_call(
         solve_kernel,
-        out_shape=jax.ShapeDtypeStruct((512, 512), BF),
+        out_shape=(
+            jax.ShapeDtypeStruct((512, 1024), BF),
+            jax.ShapeDtypeStruct((512, 512), BF),
+        ),
         in_specs=[VMEM] * 9,
-        out_specs=VMEM,
+        out_specs=(VMEM, VMEM),
         scratch_shapes=[pltpu.VMEM((512, 512), BF), pltpu.VMEM((512, 512), BF)],
-        compiler_params=grant(6),
-        cost_estimate=cost(270_000_000, 2_000_000),
+        compiler_params=grant(8),
+        cost_estimate=cost(270_000_000, 4_000_000),
         name="solve",
     )(*pieces, inverse)
 
 
-def update_kernel(g, p0, p1, p2, p3, p4, p5, p6, p7, right, y, slab, rhs,
-                  slab_out, rhs_out, wide, slab_v, rhs_v, sems):
-    pieces = (p0, p1, p2, p3, p4, p5, p6, p7)
+def update_kernel(k0, k1, k2, k3, bases, middle, right, y, slab, rhs,
+                  slab_out, rhs_out, g, wide, slab_v, rhs_v, sems):
     tile = 512
-    for j in range(4):
-        core = jnp.concatenate([p[:, j * 256 : (j + 1) * 256] for p in pieces], axis=0)
+    for i in range(2):
+        rows = slice(i * tile, (i + 1) * tile)
+        left = jnp.concatenate([k[:, i * 256 : (i + 1) * 256] for k in (k0, k1, k2, k3)], axis=0)
+        g[rows, :] = dot_t(bases[rows, :], left).astype(BF)
+    for j in range(4):
         for i in range(2):
             rows = slice(i * tile, (i + 1) * tile)
-            wide[j, rows, :] = dot(g[rows, :], core).astype(BF)
+            wide[j, rows, :] = dot(g[rows, :], middle[:, j * 256 : (j + 1) * 256]).astype(BF)
     stores = []
     for j in range(4):
         cols = slice(j * tile, (j + 1) * tile)
@@ -237,25 +217,26 @@
         copy.wait()
 
 
-def update(g, pieces, right, y, slab, rhs):
+def update(lefts, bases, middle, right, y, slab, rhs):
     return pl.pallas_call(
         update_kernel,
         out_shape=(
             jax.ShapeDtypeStruct((1024, 2048), BF),
             jax.ShapeDtypeStruct((1024, 512), BF),
         ),
-        in_specs=[VMEM] * 13,
+        in_specs=[VMEM] * 10,
         out_specs=(HBM, HBM),
         scratch_shapes=[
+            pltpu.VMEM((1024, 512), BF),
             pltpu.VMEM((4, 1024, 256), BF),
             pltpu.VMEM((1024, 2048), BF),
             pltpu.VMEM((1024, 512), BF),
             pltpu.SemaphoreType.DMA((5,)),
         ],
-        compiler_params=grant(24),
-        cost_estimate=cost(2_700_000_000, 12_000_000),
+        compiler_params=grant(26),
+        cost_estimate=cost(3_000_000_000, 12_000_000),
         name="update",
-    )(g, *pieces, right, y, slab, rhs)
+    )(*lefts, bases, middle, right, y, slab, rhs)
 
 
 def per_device(
@@ -281,9 +262,9 @@
     left_part = join((part, part_far))
     lefts = [left_part] + [exchange(left_part, x=d) for d in (1, 2, 3)]
     twins = [exchange(p, core=1) for p in pieces]
-    y = solve(pieces + twins, inverse)
-    g = left_product(lefts, bases)
-    return update(g, pieces + twins, right, y, slab, rhs)
+    middle, y = solve(pieces + twins, inverse)
+    lefts = [lefts[n] for n in (0, 2, 3, 1)]
+    return update(lefts, bases, middle, right, y, slab, rhs)
 
 
 def solution(mesh):

time: 38.8 us -> 48.3 us (1.24)
  the two profiles are of different devices: /device:TPU:62 before, /device:TPU:24 now
where the time goes in v3:
time: 48.3 us; the launch traced here: 48.2 us
  starting transfers between devices  20.6 us (43%)
  waiting for transfers between devices  18.9 us (39%)
  Pallas kernels  7.94 us (16%)
  between operations  0.72 us (1%)
    ppermute x14, starting transfers between devices, exchange(): return lax.ppermute(array, ('row', 'col'), pairs)  20.6 us
    ppermute x14, waiting for transfers between devices, exchange(): return lax.ppermute(array, ('row', 'col'), pairs)  18.9 us
    pallas_call x1, Pallas kernels, update(): pl.pallas_call(update_kernel, out_shape=(jax.ShapeDtypeStruct((1024, 2048...  4.23 us
    pallas_call x1, Pallas kernels, project(): pl.pallas_call(project_kernel, out_shape=(jax.ShapeDtypeStruct((16, 1536)...  2.01 us
    pallas_call x1, Pallas kernels, load(): pl.pallas_call(load_kernel, out_shape=[jax.ShapeDtypeStruct(a.shape, a.dt...  1.05 us
  transfers between devices with their start and end apart: 14, of which 6 were waited for; matrix products, arithmetic and copies ran while one was open for 0% of the time, Pallas kernels for 4%

profile of v3, /device:TPU:24, one launch (start us, length us, event | category | flops | bytes accessed | tf_op | source)
XLA Modules:
  0.0 48.2 jit_solution(7902868521721526543)
XLA Ops:
  0.6 0.0 copy-start.1
  0.6 0.0 copy-start
  0.7 2.0 %project.1 = (bf16[16,1536]{1,0:T(8,128)(2,1)S(1)}, bf16[64,512]{1,0:T(8,128)(2,1)S(1)}, bf16[1024,256]{1,0:T(8,128)(2,1)S(1)}, bf16[2048,256]{1,0:T(8,128)(2,1)S(1)}) custom-call(s32[4]{0:T(128)} %ranks_h.1, s32[2]{0:T(128)} %rows_h.1, bf16[64,1024]{1,0:T(8,128)(2,1)} %bitcast.1, bf16[1024,256]{1,0:T(8,128)(2,1)} %bases_h.1, bf16[16,2048]{1,0:T(8,128)(2,1)} %top_h.1, ...), custom_call_target="tpu_custom_call" | custom-call | flops 50000000 | bytes 1800000 | tf_op jit(solution)/shard_map/project/pallas_call | solution.py:81
  2.7 4.7 %collective-permute-start.6 = (bf16[16,1536]{1,0:T(8,128)(2,1)S(1)}, bf16[16,1536]{1,0:T(8,128)(2,1)S(1)}, u32[]{:S(2)}, u32[]{:S(2)}) collective-permute-start(bf16[16,1536]{1,0:T(8,128)(2,1)S(1)} %get-tuple-element.10.refs_0_), channel_id=1, source_target_pairs={{0,192},{1,193},{2,194},{3,195},{4,196},{5,197},{6,198},{7,199},{8... | collective-permute-start | bytes 147464 | tf_op jit(solution)/shard_map/ppermute | solution.py:32
  7.4 0.0 collective-permute-start.5
  7.4 0.7 %collective-permute-start.4 = (bf16[16,1536]{1,0:T(8,128)(2,1)S(1)}, bf16[16,1536]{1,0:T(8,128)(2,1)S(1)}, u32[]{:S(2)}, u32[]{:S(2)}) collective-permute-start(bf16[16,1536]{1,0:T(8,128)(2,1)S(1)} %get-tuple-element.10.refs_0_), channel_id=1, source_target_pairs={{0,64},{1,65},{2,66},{3,67},{4,68},{5,69},{6,70},{7,71},{8,72},{9,... | collective-permute-start | bytes 147464 | tf_op jit(solution)/shard_map/ppermute | solution.py:32
  8.0 1.8 %collective-permute-done.6.refs_3_ = bf16[16,1536]{1,0:T(8,128)(2,1)S(1)} collective-permute-done((bf16[16,1536]{1,0:T(8,128)(2,1)S(1)}, bf16[16,1536]{1,0:T(8,128)(2,1)S(1)}, u32[]{:S(2)}, u32[]{:S(2)}) %collective-permute-start.6) | collective-permute-done | bytes 49184 | tf_op jit(solution)/shard_map/ppermute | solution.py:32
  9.8 2.5 %collective-permute-done.5.refs_2_ = bf16[16,1536]{1,0:T(8,128)(2,1)S(1)} collective-permute-done((bf16[16,1536]{1,0:T(8,128)(2,1)S(1)}, bf16[16,1536]{1,0:T(8,128)(2,1)S(1)}, u32[]{:S(2)}, u32[]{:S(2)}) %collective-permute-start.5) | collective-permute-done | bytes 49184 | tf_op jit(solution)/shard_map/ppermute | solution.py:32
  12.4 0.0 collective-permute-done.4.refs_1_
  12.4 0.4 collective-permute-start.9
  12.8 2.5 %collective-permute-start.8 = (bf16[64,1536]{1,0:T(8,128)(2,1)S(1)}, bf16[64,1536]{1,0:T(8,128)(2,1)S(1)}, u32[]{:S(2)}, u32[]{:S(2)}) collective-permute-start(bf16[64,1536]{1,0:T(8,128)(2,1)S(1)} %shard_map.114.p0), channel_id=1, source_target_pairs={{0,32},{1,33},{2,34},{3,35},{4,36},{5,37},{6,38},{7,39},{8,40},{9,... | collective-permute-start | bytes 589832 | tf_op jit(solution)/shard_map/ppermute | solution.py:32
  15.3 1.3 %collective-permute-start.7 = (bf16[64,1536]{1,0:T(8,128)(2,1)S(1)}, bf16[64,1536]{1,0:T(8,128)(2,1)S(1)}, u32[]{:S(2)}, u32[]{:S(2)}) collective-permute-start(bf16[64,1536]{1,0:T(8,128)(2,1)S(1)} %shard_map.114.p0), channel_id=1, source_target_pairs={{0,16},{1,17},{2,18},{3,19},{4,20},{5,21},{6,22},{7,23},{8,24},{9,... | collective-permute-start | bytes 589832 | tf_op jit(solution)/shard_map/ppermute | solution.py:32
  16.6 0.0 collective-permute-start.10
  16.6 7.2 %collective-permute-done.9.p3 = bf16[64,1536]{1,0:T(8,128)(2,1)S(1)} collective-permute-done((bf16[64,1536]{1,0:T(8,128)(2,1)S(1)}, bf16[64,1536]{1,0:T(8,128)(2,1)S(1)}, u32[]{:S(2)}, u32[]{:S(2)}) %collective-permute-start.9) | collective-permute-done | bytes 196640 | tf_op jit(solution)/shard_map/ppermute | solution.py:32
  23.7 0.0 collective-permute-start.13
  23.7 0.0 collective-permute-done.8.p2
  23.8 0.5 %collective-permute-start.12 = (bf16[64,1536]{1,0:T(8,128)(2,1)S(1)}, bf16[64,1536]{1,0:T(8,128)(2,1)S(1)}, u32[]{:S(2)}, u32[]{:S(2)}) collective-permute-start(bf16[64,1536]{1,0:T(8,128)(2,1)S(1)} %collective-permute-done.8.p2), channel_id=1, source_target_pairs={{0,8},{1,9},{2,10},{3,11},{4,12},{5,13},{6,14},{7,15},{8,0},{9,1},... | collective-permute-start | bytes 589832 | tf_op jit(solution)/shard_map/ppermute | solution.py:32
  24.3 0.1 collective-permute-done.7.p1
  24.4 0.0 collective-permute-start.11
  24.4 6.1 %collective-permute-start = (bf16[64,512]{1,0:T(8,128)(2,1)S(1)}, bf16[64,512]{1,0:T(8,128)(2,1)S(1)}, u32[]{:S(2)}, u32[]{:S(2)}) collective-permute-start(bf16[64,512]{1,0:T(8,128)(2,1)S(1)} %get-tuple-element.8.refs_0_), channel_id=1, source_target_pairs={{0,4},{1,5},{2,6},{3,7},{4,0},{5,1},{6,2},{7,3},{8,12},{9,13},{10,... | collective-permute-start | bytes 196616 | tf_op jit(solution)/shard_map/ppermute | solution.py:32
  30.5 2.8 %collective-permute-done.refs_1_ = bf16[64,512]{1,0:T(8,128)(2,1)S(1)} collective-permute-done((bf16[64,512]{1,0:T(8,128)(2,1)S(1)}, bf16[64,512]{1,0:T(8,128)(2,1)S(1)}, u32[]{:S(2)}, u32[]{:S(2)}) %collective-permute-start) | collective-permute-done | bytes 65568 | tf_op jit(solution)/shard_map/ppermute | solution.py:32
  33.3 1.6 %collective-permute-start.3 = (bf16[128,512]{1,0:T(8,128)(2,1)S(1)}, bf16[128,512]{1,0:T(8,128)(2,1)S(1)}, u32[]{:S(2)}, u32[]{:S(2)}) collective-permute-start(bf16[128,512]{1,0:T(8,128)(2,1)S(1)} %shard_map.113.k0), channel_id=1, source_target_pairs={{0,1},{1,0},{2,3},{3,2},{4,5},{5,4},{6,7},{7,6},{8,9},{9,8},{10,11... | collective-permute-start | bytes 393224 | tf_op jit(solution)/shard_map/ppermute | solution.py:32
  34.9 0.0 collective-permute-done.10.p4
  34.9 2.1 %collective-permute-start.2 = (bf16[128,512]{1,0:T(8,128)(2,1)S(1)}, bf16[128,512]{1,0:T(8,128)(2,1)S(1)}, u32[]{:S(2)}, u32[]{:S(2)}) collective-permute-start(bf16[128,512]{1,0:T(8,128)(2,1)S(1)} %shard_map.113.k0), channel_id=1, source_target_pairs={{0,3},{1,2},{2,1},{3,0},{4,7},{5,6},{6,5},{7,4},{8,11},{9,10},{10,... | collective-permute-start | bytes 393224 | tf_op jit(solution)/shard_map/ppermute | solution.py:32
  37.0 0.0 collective-permute-done.13.p7
  37.0 0.7 %collective-permute-start.1 = (bf16[128,512]{1,0:T(8,128)(2,1)S(1)}, bf16[128,512]{1,0:T(8,128)(2,1)S(1)}, u32[]{:S(2)}, u32[]{:S(2)}) collective-permute-start(bf16[128,512]{1,0:T(8,128)(2,1)S(1)} %shard_map.113.k0), channel_id=1, source_target_pairs={{0,2},{1,3},{2,0},{3,1},{4,6},{5,7},{6,4},{7,5},{8,10},{9,11},{10,... | collective-permute-start | bytes 393224 | tf_op jit(solution)/shard_map/ppermute | solution.py:32
  37.7 1.0 %shard_map.115.inverse = bf16[512,512]{1,0:T(8,128)(2,1)S(1)} custom-call(bf16[512,512]{1,0:T(8,128)(2,1)} %refs_0_.1), custom_call_target="tpu_custom_call" | custom-call | bytes 8000000 | tf_op jit(solution)/shard_map/pallas_call | solution.py:112
  38.8 0.0 collective-permute-done.12.p6
  38.8 0.0 collective-permute-done.11.p5
  38.8 0.6 %solve.1 = (bf16[512,1024]{1,0:T(8,128)(2,1)S(1)}, bf16[512,512]{1,0:T(8,128)(2,1)S(1)}) custom-call(bf16[64,1536]{1,0:T(8,128)(2,1)S(1)} %shard_map.114.p0, bf16[64,1536]{1,0:T(8,128)(2,1)S(1)} %collective-permute-done.7.p1, bf16[64,1536]{1,0:T(8,128)(2,1)S(1)} %collective-permute-done.8.p2, bf16[64,1536]{1,0:T(8,128)(2,1)S(1)} %collective-permute-done.9.p3, ...), custom_call_target="tpu_custom_call" | custom-call | flops 270000000 | bytes 4000000 | tf_op jit(solution)/shard_map/solve/pallas_call | solution.py:180
  39.4 0.0 collective-permute-done.3.k3
  39.4 4.5 %collective-permute-done.2.k2 = bf16[128,512]{1,0:T(8,128)(2,1)S(1)} collective-permute-done((bf16[128,512]{1,0:T(8,128)(2,1)S(1)}, bf16[128,512]{1,0:T(8,128)(2,1)S(1)}, u32[]{:S(2)}, u32[]{:S(2)}) %collective-permute-start.2) | collective-permute-done | bytes 131104 | tf_op jit(solution)/shard_map/ppermute | solution.py:32
  43.9 0.0 collective-permute-done.1.k1
  43.9 0.0 copy-done.1
  43.9 0.0 copy-done
  43.9 4.2 %update.1 = (bf16[1024,2048]{1,0:T(8,128)(2,1)}, bf16[1024,512]{1,0:T(8,128)(2,1)}) custom-call(bf16[128,512]{1,0:T(8,128)(2,1)S(1)} %shard_map.113.k0, bf16[128,512]{1,0:T(8,128)(2,1)S(1)} %collective-permute-done.1.k1, bf16[128,512]{1,0:T(8,128)(2,1)S(1)} %collective-permute-done.2.k2, bf16[128,512]{1,0:T(8,128)(2,1)S(1)} %collective-permute-done.3.k3, ...), custom_call_target="tpu_custom_call" | custom-call | flops 3000000000 | bytes 12000000 | tf_op jit(solution)/shard_map/update/pallas_call | solution.py:221
  (2 shorter events, 0.0 us)
Async XLA Ops:
  0.6 43.3 %copy-start.1 = (bf16[1024,512]{1,0:T(8,128)(2,1)S(1)}, bf16[1024,512]{1,0:T(8,128)(2,1)}, u32[]{:S(2)}) copy-start(bf16[1024,512]{1,0:T(8,128)(2,1)} %rhs.1) | copy-start | bytes 3145732
  0.6 43.3 %copy-start = (bf16[1024,2048]{1,0:T(8,128)(2,1)S(1)}, bf16[1024,2048]{1,0:T(8,128)(2,1)}, u32[]{:S(2)}) copy-start(bf16[1024,2048]{1,0:T(8,128)(2,1)} %slab.1) | copy-start | bytes 12582916
  2.7 7.2 %collective-permute-start.6 = (bf16[16,1536]{1,0:T(8,128)(2,1)S(1)}, bf16[16,1536]{1,0:T(8,128)(2,1)S(1)}, u32[]{:S(2)}, u32[]{:S(2)}) collective-permute-start(bf16[16,1536]{1,0:T(8,128)(2,1)S(1)} %get-tuple-element.10.refs_0_), channel_id=1, source_target_pairs={{0,192},{1,193},{2,194},{3,195},{4,196},{5,197},{6,198},{7,199},{8... | collective-permute-start | bytes 147464 | tf_op jit(solution)/shard_map/ppermute | solution.py:32
  7.4 5.0 %collective-permute-start.5 = (bf16[16,1536]{1,0:T(8,128)(2,1)S(1)}, bf16[16,1536]{1,0:T(8,128)(2,1)S(1)}, u32[]{:S(2)}, u32[]{:S(2)}) collective-permute-start(bf16[16,1536]{1,0:T(8,128)(2,1)S(1)} %get-tuple-element.10.refs_0_), channel_id=1, source_target_pairs={{0,128},{1,129},{2,130},{3,131},{4,132},{5,133},{6,134},{7,135},{8... | collective-permute-start | bytes 147464 | tf_op jit(solution)/shard_map/ppermute | solution.py:32
  7.4 5.0 %collective-permute-start.4 = (bf16[16,1536]{1,0:T(8,128)(2,1)S(1)}, bf16[16,1536]{1,0:T(8,128)(2,1)S(1)}, u32[]{:S(2)}, u32[]{:S(2)}) collective-permute-start(bf16[16,1536]{1,0:T(8,128)(2,1)S(1)} %get-tuple-element.10.refs_0_), channel_id=1, source_target_pairs={{0,64},{1,65},{2,66},{3,67},{4,68},{5,69},{6,70},{7,71},{8,72},{9,... | collective-permute-start | bytes 147464 | tf_op jit(solution)/shard_map/ppermute | solution.py:32
  12.4 11.4 %collective-permute-start.9 = (bf16[64,1536]{1,0:T(8,128)(2,1)S(1)}, bf16[64,1536]{1,0:T(8,128)(2,1)S(1)}, u32[]{:S(2)}, u32[]{:S(2)}) collective-permute-start(bf16[64,1536]{1,0:T(8,128)(2,1)S(1)} %shard_map.114.p0), channel_id=1, source_target_pairs={{0,48},{1,49},{2,50},{3,51},{4,52},{5,53},{6,54},{7,55},{8,56},{9,... | collective-permute-start | bytes 589832 | tf_op jit(solution)/shard_map/ppermute | solution.py:32
  12.8 11.0 %collective-permute-start.8 = (bf16[64,1536]{1,0:T(8,128)(2,1)S(1)}, bf16[64,1536]{1,0:T(8,128)(2,1)S(1)}, u32[]{:S(2)}, u32[]{:S(2)}) collective-permute-start(bf16[64,1536]{1,0:T(8,128)(2,1)S(1)} %shard_map.114.p0), channel_id=1, source_target_pairs={{0,32},{1,33},{2,34},{3,35},{4,36},{5,37},{6,38},{7,39},{8,40},{9,... | collective-permute-start | bytes 589832 | tf_op jit(solution)/shard_map/ppermute | solution.py:32
  15.3 9.1 %collective-permute-start.7 = (bf16[64,1536]{1,0:T(8,128)(2,1)S(1)}, bf16[64,1536]{1,0:T(8,128)(2,1)S(1)}, u32[]{:S(2)}, u32[]{:S(2)}) collective-permute-start(bf16[64,1536]{1,0:T(8,128)(2,1)S(1)} %shard_map.114.p0), channel_id=1, source_target_pairs={{0,16},{1,17},{2,18},{3,19},{4,20},{5,21},{6,22},{7,23},{8,24},{9,... | collective-permute-start | bytes 589832 | tf_op jit(solution)/shard_map/ppermute | solution.py:32
  16.6 18.3 %collective-permute-start.10 = (bf16[64,1536]{1,0:T(8,128)(2,1)S(1)}, bf16[64,1536]{1,0:T(8,128)(2,1)S(1)}, u32[]{:S(2)}, u32[]{:S(2)}) collective-permute-start(bf16[64,1536]{1,0:T(8,128)(2,1)S(1)} %shard_map.114.p0), channel_id=1, source_target_pairs={{0,8},{1,9},{2,10},{3,11},{4,12},{5,13},{6,14},{7,15},{8,0},{9,1},... | collective-permute-start | bytes 589832 | tf_op jit(solution)/shard_map/ppermute | solution.py:32
  23.7 13.2 %collective-permute-start.13 = (bf16[64,1536]{1,0:T(8,128)(2,1)S(1)}, bf16[64,1536]{1,0:T(8,128)(2,1)S(1)}, u32[]{:S(2)}, u32[]{:S(2)}) collective-permute-start(bf16[64,1536]{1,0:T(8,128)(2,1)S(1)} %collective-permute-done.9.p3), channel_id=1, source_target_pairs={{0,8},{1,9},{2,10},{3,11},{4,12},{5,13},{6,14},{7,15},{8,0},{9,1},... | collective-permute-start | bytes 589832 | tf_op jit(solution)/shard_map/ppermute | solution.py:32
  23.8 15.0 %collective-permute-start.12 = (bf16[64,1536]{1,0:T(8,128)(2,1)S(1)}, bf16[64,1536]{1,0:T(8,128)(2,1)S(1)}, u32[]{:S(2)}, u32[]{:S(2)}) collective-permute-start(bf16[64,1536]{1,0:T(8,128)(2,1)S(1)} %collective-permute-done.8.p2), channel_id=1, source_target_pairs={{0,8},{1,9},{2,10},{3,11},{4,12},{5,13},{6,14},{7,15},{8,0},{9,1},... | collective-permute-start | bytes 589832 | tf_op jit(solution)/shard_map/ppermute | solution.py:32
  24.4 14.4 %collective-permute-start.11 = (bf16[64,1536]{1,0:T(8,128)(2,1)S(1)}, bf16[64,1536]{1,0:T(8,128)(2,1)S(1)}, u32[]{:S(2)}, u32[]{:S(2)}) collective-permute-start(bf16[64,1536]{1,0:T(8,128)(2,1)S(1)} %collective-permute-done.7.p1), channel_id=1, source_target_pairs={{0,8},{1,9},{2,10},{3,11},{4,12},{5,13},{6,14},{7,15},{8,0},{9,1},... | collective-permute-start | bytes 589832 | tf_op jit(solution)/shard_map/ppermute | solution.py:32
  24.4 8.9 %collective-permute-start = (bf16[64,512]{1,0:T(8,128)(2,1)S(1)}, bf16[64,512]{1,0:T(8,128)(2,1)S(1)}, u32[]{:S(2)}, u32[]{:S(2)}) collective-permute-start(bf16[64,512]{1,0:T(8,128)(2,1)S(1)} %get-tuple-element.8.refs_0_), channel_id=1, source_target_pairs={{0,4},{1,5},{2,6},{3,7},{4,0},{5,1},{6,2},{7,3},{8,12},{9,13},{10,... | collective-permute-start | bytes 196616 | tf_op jit(solution)/shard_map/ppermute | solution.py:32
  33.3 6.1 %collective-permute-start.3 = (bf16[128,512]{1,0:T(8,128)(2,1)S(1)}, bf16[128,512]{1,0:T(8,128)(2,1)S(1)}, u32[]{:S(2)}, u32[]{:S(2)}) collective-permute-start(bf16[128,512]{1,0:T(8,128)(2,1)S(1)} %shard_map.113.k0), channel_id=1, source_target_pairs={{0,1},{1,0},{2,3},{3,2},{4,5},{5,4},{6,7},{7,6},{8,9},{9,8},{10,11... | collective-permute-start | bytes 393224 | tf_op jit(solution)/shard_map/ppermute | solution.py:32
  34.9 9.1 %collective-permute-start.2 = (bf16[128,512]{1,0:T(8,128)(2,1)S(1)}, bf16[128,512]{1,0:T(8,128)(2,1)S(1)}, u32[]{:S(2)}, u32[]{:S(2)}) collective-permute-start(bf16[128,512]{1,0:T(8,128)(2,1)S(1)} %shard_map.113.k0), channel_id=1, source_target_pairs={{0,3},{1,2},{2,1},{3,0},{4,7},{5,6},{6,5},{7,4},{8,11},{9,10},{10,... | collective-permute-start | bytes 393224 | tf_op jit(solution)/shard_map/ppermute | solution.py:32
  37.0 7.0 %collective-permute-start.1 = (bf16[128,512]{1,0:T(8,128)(2,1)S(1)}, bf16[128,512]{1,0:T(8,128)(2,1)S(1)}, u32[]{:S(2)}, u32[]{:S(2)}) collective-permute-start(bf16[128,512]{1,0:T(8,128)(2,1)S(1)} %shard_map.113.k0), channel_id=1, source_target_pairs={{0,2},{1,3},{2,0},{3,1},{4,6},{5,7},{6,4},{7,5},{8,10},{9,11},{10,... | collective-permute-start | bytes 393224 | tf_op jit(solution)/shard_map/ppermute | solution.py:32

commit v4 on v3

--- a/solution.py
+++ b/solution.py
@@ -63,13 +63,16 @@
         part = slice(i * tile, (i + 1) * tile)
         sources.append((bases_h.at[part], bases.at[part]))
     sources.append((pivot_h, pack.at[:, 1024:]))
-    for copy in start_all(sources, sems):
+    copies = start_all(sources, sems)
+    for copy in copies[:7]:
         copy.wait()
     lane = lax.broadcasted_iota(jnp.int32, (16, 256), 1)
     for j in range(4):
         part = dot(top[:, j * tile : (j + 1) * tile], right[j * tile : (j + 1) * tile, :])
         part = jnp.where(lane < ranks[j], part, 0.0)
         pack[:, j * 256 : (j + 1) * 256] = part.astype(BF)
+    for copy in copies[7:]:
+        copy.wait()
     lane = lax.broadcasted_iota(jnp.int32, (64, 256), 1)
     for i in range(2):
         part = dot(left[:, i * tile : (i + 1) * tile], bases[i * tile : (i + 1) * tile, :])

time: 48.3 us -> 48.2 us (level)
  the two profiles are of different devices: /device:TPU:24 before, /device:TPU:8 now
where the time goes in v4:
time: 48.2 us; the launch traced here: 48.1 us
  starting transfers between devices  20.1 us (42%)
  waiting for transfers between devices  19.4 us (40%)
  Pallas kernels  7.87 us (16%)
  between operations  0.72 us (1%)
    ppermute x14, starting transfers between devices, exchange(): return lax.ppermute(array, ('row', 'col'), pairs)  20.1 us
    ppermute x14, waiting for transfers between devices, exchange(): return lax.ppermute(array, ('row', 'col'), pairs)  19.4 us
    pallas_call x1, Pallas kernels, update(): pl.pallas_call(update_kernel, out_shape=(jax.ShapeDtypeStruct((1024, 2048...  4.23 us
    pallas_call x1, Pallas kernels, project(): pl.pallas_call(project_kernel, out_shape=(jax.ShapeDtypeStruct((16, 1536)...  1.93 us
    pallas_call x1, Pallas kernels, load(): pl.pallas_call(load_kernel, out_shape=[jax.ShapeDtypeStruct(a.shape, a.dt...  1.05 us
  transfers between devices with their start and end apart: 14, of which 7 were waited for; matrix products, arithmetic and copies ran while one was open for 0% of the time, Pallas kernels for 4%

profile of v4, /device:TPU:8, one launch (start us, length us, event | category | flops | bytes accessed | tf_op | source)
XLA Modules:
  0.0 48.1 jit_solution(15846496983888408495)
XLA Ops:
  0.6 0.0 copy-start.1
  0.6 0.0 copy-start
  0.7 1.9 %project.1 = (bf16[16,1536]{1,0:T(8,128)(2,1)S(1)}, bf16[64,512]{1,0:T(8,128)(2,1)S(1)}, bf16[1024,256]{1,0:T(8,128)(2,1)S(1)}, bf16[2048,256]{1,0:T(8,128)(2,1)S(1)}) custom-call(s32[4]{0:T(128)} %ranks_h.1, s32[2]{0:T(128)} %rows_h.1, bf16[64,1024]{1,0:T(8,128)(2,1)} %bitcast.1, bf16[1024,256]{1,0:T(8,128)(2,1)} %bases_h.1, bf16[16,2048]{1,0:T(8,128)(2,1)} %top_h.1, ...), custom_call_target="tpu_custom_call" | custom-call | flops 50000000 | bytes 1800000 | tf_op jit(solution)/shard_map/project/pallas_call | solution.py:84
  2.6 4.7 %collective-permute-start.6 = (bf16[16,1536]{1,0:T(8,128)(2,1)S(1)}, bf16[16,1536]{1,0:T(8,128)(2,1)S(1)}, u32[]{:S(2)}, u32[]{:S(2)}) collective-permute-start(bf16[16,1536]{1,0:T(8,128)(2,1)S(1)} %get-tuple-element.10.refs_0_), channel_id=1, source_target_pairs={{0,192},{1,193},{2,194},{3,195},{4,196},{5,197},{6,198},{7,199},{8... | collective-permute-start | bytes 147464 | tf_op jit(solution)/shard_map/ppermute | solution.py:32
  7.3 0.0 collective-permute-start.5
  7.3 0.7 %collective-permute-start.4 = (bf16[16,1536]{1,0:T(8,128)(2,1)S(1)}, bf16[16,1536]{1,0:T(8,128)(2,1)S(1)}, u32[]{:S(2)}, u32[]{:S(2)}) collective-permute-start(bf16[16,1536]{1,0:T(8,128)(2,1)S(1)} %get-tuple-element.10.refs_0_), channel_id=1, source_target_pairs={{0,64},{1,65},{2,66},{3,67},{4,68},{5,69},{6,70},{7,71},{8,72},{9,... | collective-permute-start | bytes 147464 | tf_op jit(solution)/shard_map/ppermute | solution.py:32
  8.0 1.8 %collective-permute-done.6.refs_3_ = bf16[16,1536]{1,0:T(8,128)(2,1)S(1)} collective-permute-done((bf16[16,1536]{1,0:T(8,128)(2,1)S(1)}, bf16[16,1536]{1,0:T(8,128)(2,1)S(1)}, u32[]{:S(2)}, u32[]{:S(2)}) %collective-permute-start.6) | collective-permute-done | bytes 49184 | tf_op jit(solution)/shard_map/ppermute | solution.py:32
  9.8 2.5 %collective-permute-done.5.refs_2_ = bf16[16,1536]{1,0:T(8,128)(2,1)S(1)} collective-permute-done((bf16[16,1536]{1,0:T(8,128)(2,1)S(1)}, bf16[16,1536]{1,0:T(8,128)(2,1)S(1)}, u32[]{:S(2)}, u32[]{:S(2)}) %collective-permute-start.5) | collective-permute-done | bytes 49184 | tf_op jit(solution)/shard_map/ppermute | solution.py:32
  12.3 0.0 collective-permute-done.4.refs_1_
  12.3 1.7 %collective-permute-start.9 = (bf16[64,1536]{1,0:T(8,128)(2,1)S(1)}, bf16[64,1536]{1,0:T(8,128)(2,1)S(1)}, u32[]{:S(2)}, u32[]{:S(2)}) collective-permute-start(bf16[64,1536]{1,0:T(8,128)(2,1)S(1)} %shard_map.114.p0), channel_id=1, source_target_pairs={{0,48},{1,49},{2,50},{3,51},{4,52},{5,53},{6,54},{7,55},{8,56},{9,... | collective-permute-start | bytes 589832 | tf_op jit(solution)/shard_map/ppermute | solution.py:32
  14.0 1.0 %collective-permute-start.8 = (bf16[64,1536]{1,0:T(8,128)(2,1)S(1)}, bf16[64,1536]{1,0:T(8,128)(2,1)S(1)}, u32[]{:S(2)}, u32[]{:S(2)}) collective-permute-start(bf16[64,1536]{1,0:T(8,128)(2,1)S(1)} %shard_map.114.p0), channel_id=1, source_target_pairs={{0,32},{1,33},{2,34},{3,35},{4,36},{5,37},{6,38},{7,39},{8,40},{9,... | collective-permute-start | bytes 589832 | tf_op jit(solution)/shard_map/ppermute | solution.py:32
  15.0 1.5 %collective-permute-start.7 = (bf16[64,1536]{1,0:T(8,128)(2,1)S(1)}, bf16[64,1536]{1,0:T(8,128)(2,1)S(1)}, u32[]{:S(2)}, u32[]{:S(2)}) collective-permute-start(bf16[64,1536]{1,0:T(8,128)(2,1)S(1)} %shard_map.114.p0), channel_id=1, source_target_pairs={{0,16},{1,17},{2,18},{3,19},{4,20},{5,21},{6,22},{7,23},{8,24},{9,... | collective-permute-start | bytes 589832 | tf_op jit(solution)/shard_map/ppermute | solution.py:32
  16.5 0.0 collective-permute-start.10
  16.5 5.2 %collective-permute-done.9.p3 = bf16[64,1536]{1,0:T(8,128)(2,1)S(1)} collective-permute-done((bf16[64,1536]{1,0:T(8,128)(2,1)S(1)}, bf16[64,1536]{1,0:T(8,128)(2,1)S(1)}, u32[]{:S(2)}, u32[]{:S(2)}) %collective-permute-start.9) | collective-permute-done | bytes 196640 | tf_op jit(solution)/shard_map/ppermute | solution.py:32
  21.7 0.0 collective-permute-start.13
  21.7 1.5 %collective-permute-done.8.p2 = bf16[64,1536]{1,0:T(8,128)(2,1)S(1)} collective-permute-done((bf16[64,1536]{1,0:T(8,128)(2,1)S(1)}, bf16[64,1536]{1,0:T(8,128)(2,1)S(1)}, u32[]{:S(2)}, u32[]{:S(2)}) %collective-permute-start.8) | collective-permute-done | bytes 196640 | tf_op jit(solution)/shard_map/ppermute | solution.py:32
  23.2 0.0 collective-permute-start.12
  23.2 1.1 %collective-permute-done.7.p1 = bf16[64,1536]{1,0:T(8,128)(2,1)S(1)} collective-permute-done((bf16[64,1536]{1,0:T(8,128)(2,1)S(1)}, bf16[64,1536]{1,0:T(8,128)(2,1)S(1)}, u32[]{:S(2)}, u32[]{:S(2)}) %collective-permute-start.7) | collective-permute-done | bytes 196640 | tf_op jit(solution)/shard_map/ppermute | solution.py:32
  24.3 0.0 collective-permute-start.11
  24.3 6.1 %collective-permute-start = (bf16[64,512]{1,0:T(8,128)(2,1)S(1)}, bf16[64,512]{1,0:T(8,128)(2,1)S(1)}, u32[]{:S(2)}, u32[]{:S(2)}) collective-permute-start(bf16[64,512]{1,0:T(8,128)(2,1)S(1)} %get-tuple-element.8.refs_0_), channel_id=1, source_target_pairs={{0,4},{1,5},{2,6},{3,7},{4,0},{5,1},{6,2},{7,3},{8,12},{9,13},{10,... | collective-permute-start | bytes 196616 | tf_op jit(solution)/shard_map/ppermute | solution.py:32
  30.4 2.8 %collective-permute-done.refs_1_ = bf16[64,512]{1,0:T(8,128)(2,1)S(1)} collective-permute-done((bf16[64,512]{1,0:T(8,128)(2,1)S(1)}, bf16[64,512]{1,0:T(8,128)(2,1)S(1)}, u32[]{:S(2)}, u32[]{:S(2)}) %collective-permute-start) | collective-permute-done | bytes 65568 | tf_op jit(solution)/shard_map/ppermute | solution.py:32
  33.2 1.6 %collective-permute-start.3 = (bf16[128,512]{1,0:T(8,128)(2,1)S(1)}, bf16[128,512]{1,0:T(8,128)(2,1)S(1)}, u32[]{:S(2)}, u32[]{:S(2)}) collective-permute-start(bf16[128,512]{1,0:T(8,128)(2,1)S(1)} %shard_map.113.k0), channel_id=1, source_target_pairs={{0,1},{1,0},{2,3},{3,2},{4,5},{5,4},{6,7},{7,6},{8,9},{9,8},{10,11... | collective-permute-start | bytes 393224 | tf_op jit(solution)/shard_map/ppermute | solution.py:32
  34.8 0.0 collective-permute-done.10.p4
  34.8 2.1 %collective-permute-start.2 = (bf16[128,512]{1,0:T(8,128)(2,1)S(1)}, bf16[128,512]{1,0:T(8,128)(2,1)S(1)}, u32[]{:S(2)}, u32[]{:S(2)}) collective-permute-start(bf16[128,512]{1,0:T(8,128)(2,1)S(1)} %shard_map.113.k0), channel_id=1, source_target_pairs={{0,3},{1,2},{2,1},{3,0},{4,7},{5,6},{6,5},{7,4},{8,11},{9,10},{10,... | collective-permute-start | bytes 393224 | tf_op jit(solution)/shard_map/ppermute | solution.py:32
  36.9 0.0 collective-permute-done.13.p7
  36.9 0.7 %collective-permute-start.1 = (bf16[128,512]{1,0:T(8,128)(2,1)S(1)}, bf16[128,512]{1,0:T(8,128)(2,1)S(1)}, u32[]{:S(2)}, u32[]{:S(2)}) collective-permute-start(bf16[128,512]{1,0:T(8,128)(2,1)S(1)} %shard_map.113.k0), channel_id=1, source_target_pairs={{0,2},{1,3},{2,0},{3,1},{4,6},{5,7},{6,4},{7,5},{8,10},{9,11},{10,... | collective-permute-start | bytes 393224 | tf_op jit(solution)/shard_map/ppermute | solution.py:32
  37.6 1.0 %shard_map.115.inverse = bf16[512,512]{1,0:T(8,128)(2,1)S(1)} custom-call(bf16[512,512]{1,0:T(8,128)(2,1)} %refs_0_.1), custom_call_target="tpu_custom_call" | custom-call | bytes 8000000 | tf_op jit(solution)/shard_map/pallas_call | solution.py:115
  38.7 0.0 collective-permute-done.12.p6
  38.7 0.0 collective-permute-done.11.p5
  38.7 0.6 %solve.1 = (bf16[512,1024]{1,0:T(8,128)(2,1)S(1)}, bf16[512,512]{1,0:T(8,128)(2,1)S(1)}) custom-call(bf16[64,1536]{1,0:T(8,128)(2,1)S(1)} %shard_map.114.p0, bf16[64,1536]{1,0:T(8,128)(2,1)S(1)} %collective-permute-done.7.p1, bf16[64,1536]{1,0:T(8,128)(2,1)S(1)} %collective-permute-done.8.p2, bf16[64,1536]{1,0:T(8,128)(2,1)S(1)} %collective-permute-done.9.p3, ...), custom_call_target="tpu_custom_call" | custom-call | flops 270000000 | bytes 4000000 | tf_op jit(solution)/shard_map/solve/pallas_call | solution.py:183
  39.3 0.0 collective-permute-done.3.k3
  39.3 4.5 %collective-permute-done.2.k2 = bf16[128,512]{1,0:T(8,128)(2,1)S(1)} collective-permute-done((bf16[128,512]{1,0:T(8,128)(2,1)S(1)}, bf16[128,512]{1,0:T(8,128)(2,1)S(1)}, u32[]{:S(2)}, u32[]{:S(2)}) %collective-permute-start.2) | collective-permute-done | bytes 131104 | tf_op jit(solution)/shard_map/ppermute | solution.py:32
  43.9 0.0 collective-permute-done.1.k1
  43.9 0.0 copy-done.1
  43.9 0.0 copy-done
  43.9 4.2 %update.1 = (bf16[1024,2048]{1,0:T(8,128)(2,1)}, bf16[1024,512]{1,0:T(8,128)(2,1)}) custom-call(bf16[128,512]{1,0:T(8,128)(2,1)S(1)} %shard_map.113.k0, bf16[128,512]{1,0:T(8,128)(2,1)S(1)} %collective-permute-done.1.k1, bf16[128,512]{1,0:T(8,128)(2,1)S(1)} %collective-permute-done.2.k2, bf16[128,512]{1,0:T(8,128)(2,1)S(1)} %collective-permute-done.3.k3, ...), custom_call_target="tpu_custom_call" | custom-call | flops 3000000000 | bytes 12000000 | tf_op jit(solution)/shard_map/update/pallas_call | solution.py:224
  (2 shorter events, 0.0 us)
Async XLA Ops:
  0.6 43.2 %copy-start.1 = (bf16[1024,512]{1,0:T(8,128)(2,1)S(1)}, bf16[1024,512]{1,0:T(8,128)(2,1)}, u32[]{:S(2)}) copy-start(bf16[1024,512]{1,0:T(8,128)(2,1)} %rhs.1) | copy-start | bytes 3145732
  0.6 43.2 %copy-start = (bf16[1024,2048]{1,0:T(8,128)(2,1)S(1)}, bf16[1024,2048]{1,0:T(8,128)(2,1)}, u32[]{:S(2)}) copy-start(bf16[1024,2048]{1,0:T(8,128)(2,1)} %slab.1) | copy-start | bytes 12582916
  2.6 7.2 %collective-permute-start.6 = (bf16[16,1536]{1,0:T(8,128)(2,1)S(1)}, bf16[16,1536]{1,0:T(8,128)(2,1)S(1)}, u32[]{:S(2)}, u32[]{:S(2)}) collective-permute-start(bf16[16,1536]{1,0:T(8,128)(2,1)S(1)} %get-tuple-element.10.refs_0_), channel_id=1, source_target_pairs={{0,192},{1,193},{2,194},{3,195},{4,196},{5,197},{6,198},{7,199},{8... | collective-permute-start | bytes 147464 | tf_op jit(solution)/shard_map/ppermute | solution.py:32
  7.3 5.0 %collective-permute-start.5 = (bf16[16,1536]{1,0:T(8,128)(2,1)S(1)}, bf16[16,1536]{1,0:T(8,128)(2,1)S(1)}, u32[]{:S(2)}, u32[]{:S(2)}) collective-permute-start(bf16[16,1536]{1,0:T(8,128)(2,1)S(1)} %get-tuple-element.10.refs_0_), channel_id=1, source_target_pairs={{0,128},{1,129},{2,130},{3,131},{4,132},{5,133},{6,134},{7,135},{8... | collective-permute-start | bytes 147464 | tf_op jit(solution)/shard_map/ppermute | solution.py:32
  7.3 5.0 %collective-permute-start.4 = (bf16[16,1536]{1,0:T(8,128)(2,1)S(1)}, bf16[16,1536]{1,0:T(8,128)(2,1)S(1)}, u32[]{:S(2)}, u32[]{:S(2)}) collective-permute-start(bf16[16,1536]{1,0:T(8,128)(2,1)S(1)} %get-tuple-element.10.refs_0_), channel_id=1, source_target_pairs={{0,64},{1,65},{2,66},{3,67},{4,68},{5,69},{6,70},{7,71},{8,72},{9,... | collective-permute-start | bytes 147464 | tf_op jit(solution)/shard_map/ppermute | solution.py:32
  12.3 9.3 %collective-permute-start.9 = (bf16[64,1536]{1,0:T(8,128)(2,1)S(1)}, bf16[64,1536]{1,0:T(8,128)(2,1)S(1)}, u32[]{:S(2)}, u32[]{:S(2)}) collective-permute-start(bf16[64,1536]{1,0:T(8,128)(2,1)S(1)} %shard_map.114.p0), channel_id=1, source_target_pairs={{0,48},{1,49},{2,50},{3,51},{4,52},{5,53},{6,54},{7,55},{8,56},{9,... | collective-permute-start | bytes 589832 | tf_op jit(solution)/shard_map/ppermute | solution.py:32
  14.0 9.2 %collective-permute-start.8 = (bf16[64,1536]{1,0:T(8,128)(2,1)S(1)}, bf16[64,1536]{1,0:T(8,128)(2,1)S(1)}, u32[]{:S(2)}, u32[]{:S(2)}) collective-permute-start(bf16[64,1536]{1,0:T(8,128)(2,1)S(1)} %shard_map.114.p0), channel_id=1, source_target_pairs={{0,32},{1,33},{2,34},{3,35},{4,36},{5,37},{6,38},{7,39},{8,40},{9,... | collective-permute-start | bytes 589832 | tf_op jit(solution)/shard_map/ppermute | solution.py:32
  15.0 9.3 %collective-permute-start.7 = (bf16[64,1536]{1,0:T(8,128)(2,1)S(1)}, bf16[64,1536]{1,0:T(8,128)(2,1)S(1)}, u32[]{:S(2)}, u32[]{:S(2)}) collective-permute-start(bf16[64,1536]{1,0:T(8,128)(2,1)S(1)} %shard_map.114.p0), channel_id=1, source_target_pairs={{0,16},{1,17},{2,18},{3,19},{4,20},{5,21},{6,22},{7,23},{8,24},{9,... | collective-permute-start | bytes 589832 | tf_op jit(solution)/shard_map/ppermute | solution.py:32
  16.5 18.3 %collective-permute-start.10 = (bf16[64,1536]{1,0:T(8,128)(2,1)S(1)}, bf16[64,1536]{1,0:T(8,128)(2,1)S(1)}, u32[]{:S(2)}, u32[]{:S(2)}) collective-permute-start(bf16[64,1536]{1,0:T(8,128)(2,1)S(1)} %shard_map.114.p0), channel_id=1, source_target_pairs={{0,8},{1,9},{2,10},{3,11},{4,12},{5,13},{6,14},{7,15},{8,0},{9,1},... | collective-permute-start | bytes 589832 | tf_op jit(solution)/shard_map/ppermute | solution.py:32
  21.7 15.2 %collective-permute-start.13 = (bf16[64,1536]{1,0:T(8,128)(2,1)S(1)}, bf16[64,1536]{1,0:T(8,128)(2,1)S(1)}, u32[]{:S(2)}, u32[]{:S(2)}) collective-permute-start(bf16[64,1536]{1,0:T(8,128)(2,1)S(1)} %collective-permute-done.9.p3), channel_id=1, source_target_pairs={{0,8},{1,9},{2,10},{3,11},{4,12},{5,13},{6,14},{7,15},{8,0},{9,1},... | collective-permute-start | bytes 589832 | tf_op jit(solution)/shard_map/ppermute | solution.py:32
  23.2 15.5 %collective-permute-start.12 = (bf16[64,1536]{1,0:T(8,128)(2,1)S(1)}, bf16[64,1536]{1,0:T(8,128)(2,1)S(1)}, u32[]{:S(2)}, u32[]{:S(2)}) collective-permute-start(bf16[64,1536]{1,0:T(8,128)(2,1)S(1)} %collective-permute-done.8.p2), channel_id=1, source_target_pairs={{0,8},{1,9},{2,10},{3,11},{4,12},{5,13},{6,14},{7,15},{8,0},{9,1},... | collective-permute-start | bytes 589832 | tf_op jit(solution)/shard_map/ppermute | solution.py:32
  24.3 14.4 %collective-permute-start.11 = (bf16[64,1536]{1,0:T(8,128)(2,1)S(1)}, bf16[64,1536]{1,0:T(8,128)(2,1)S(1)}, u32[]{:S(2)}, u32[]{:S(2)}) collective-permute-start(bf16[64,1536]{1,0:T(8,128)(2,1)S(1)} %collective-permute-done.7.p1), channel_id=1, source_target_pairs={{0,8},{1,9},{2,10},{3,11},{4,12},{5,13},{6,14},{7,15},{8,0},{9,1},... | collective-permute-start | bytes 589832 | tf_op jit(solution)/shard_map/ppermute | solution.py:32
  24.3 8.9 %collective-permute-start = (bf16[64,512]{1,0:T(8,128)(2,1)S(1)}, bf16[64,512]{1,0:T(8,128)(2,1)S(1)}, u32[]{:S(2)}, u32[]{:S(2)}) collective-permute-start(bf16[64,512]{1,0:T(8,128)(2,1)S(1)} %get-tuple-element.8.refs_0_), channel_id=1, source_target_pairs={{0,4},{1,5},{2,6},{3,7},{4,0},{5,1},{6,2},{7,3},{8,12},{9,13},{10,... | collective-permute-start | bytes 196616 | tf_op jit(solution)/shard_map/ppermute | solution.py:32
  33.2 6.1 %collective-permute-start.3 = (bf16[128,512]{1,0:T(8,128)(2,1)S(1)}, bf16[128,512]{1,0:T(8,128)(2,1)S(1)}, u32[]{:S(2)}, u32[]{:S(2)}) collective-permute-start(bf16[128,512]{1,0:T(8,128)(2,1)S(1)} %shard_map.113.k0), channel_id=1, source_target_pairs={{0,1},{1,0},{2,3},{3,2},{4,5},{5,4},{6,7},{7,6},{8,9},{9,8},{10,11... | collective-permute-start | bytes 393224 | tf_op jit(solution)/shard_map/ppermute | solution.py:32
  34.8 9.1 %collective-permute-start.2 = (bf16[128,512]{1,0:T(8,128)(2,1)S(1)}, bf16[128,512]{1,0:T(8,128)(2,1)S(1)}, u32[]{:S(2)}, u32[]{:S(2)}) collective-permute-start(bf16[128,512]{1,0:T(8,128)(2,1)S(1)} %shard_map.113.k0), channel_id=1, source_target_pairs={{0,3},{1,2},{2,1},{3,0},{4,7},{5,6},{6,5},{7,4},{8,11},{9,10},{10,... | collective-permute-start | bytes 393224 | tf_op jit(solution)/shard_map/ppermute | solution.py:32
  36.9 7.0 %collective-permute-start.1 = (bf16[128,512]{1,0:T(8,128)(2,1)S(1)}, bf16[128,512]{1,0:T(8,128)(2,1)S(1)}, u32[]{:S(2)}, u32[]{:S(2)}) collective-permute-start(bf16[128,512]{1,0:T(8,128)(2,1)S(1)} %shard_map.113.k0), channel_id=1, source_target_pairs={{0,2},{1,3},{2,0},{3,1},{4,6},{5,7},{6,4},{7,5},{8,10},{9,11},{10,... | collective-permute-start | bytes 393224 | tf_op jit(solution)/shard_map/ppermute | solution.py:32

commit v5 on v4

--- a/solution.py
+++ b/solution.py
@@ -213,9 +213,11 @@
         slab_v[:, cols] = (slab[:, cols].astype(F32) - change).astype(BF)
         stores.append(pltpu.make_async_copy(slab_v.at[:, cols], slab_out.at[:, cols], sems.at[j]))
         stores[-1].start()
-    rhs_v[...] = (rhs[...].astype(F32) - dot(g[...], y[...])).astype(BF)
-    stores.append(pltpu.make_async_copy(rhs_v, rhs_out, sems.at[4]))
-    stores[-1].start()
+    for i in range(2):
+        rows = slice(i * tile, (i + 1) * tile)
+        rhs_v[rows, :] = (rhs[rows, :].astype(F32) - dot(g[rows, :], y[...])).astype(BF)
+        stores.append(pltpu.make_async_copy(rhs_v.at[rows], rhs_out.at[rows], sems.at[4 + i]))
+        stores[-1].start()
     for copy in stores:
         copy.wait()
 
@@ -234,7 +236,7 @@
             pltpu.VMEM((4, 1024, 256), BF),
             pltpu.VMEM((1024, 2048), BF),
             pltpu.VMEM((1024, 512), BF),
-            pltpu.SemaphoreType.DMA((5,)),
+            pltpu.SemaphoreType.DMA((6,)),
         ],
         compiler_params=grant(26),
         cost_estimate=cost(3_000_000_000, 12_000_000),

time: 48.2 us -> 48.2 us (level)
  no operation moved by 1% of the time
where the time goes in v5:
time: 48.2 us; the launch traced here: 48.1 us
  starting transfers between devices  20.1 us (42%)
  waiting for transfers between devices  19.4 us (40%)
  Pallas kernels  7.86 us (16%)
  between operations  0.72 us (1%)
    ppermute x14, starting transfers between devices, exchange(): return lax.ppermute(array, ('row', 'col'), pairs)  20.1 us
    ppermute x14, waiting for transfers between devices, exchange(): return lax.ppermute(array, ('row', 'col'), pairs)  19.4 us
    pallas_call x1, Pallas kernels, update(): pl.pallas_call(update_kernel, out_shape=(jax.ShapeDtypeStruct((1024, 2048...  4.22 us
    pallas_call x1, Pallas kernels, project(): pl.pallas_call(project_kernel, out_shape=(jax.ShapeDtypeStruct((16, 1536)...  1.93 us
    pallas_call x1, Pallas kernels, load(): pl.pallas_call(load_kernel, out_shape=[jax.ShapeDtypeStruct(a.shape, a.dt...  1.05 us
  transfers between devices with their start and end apart: 14, of which 7 were waited for; matrix products, arithmetic and copies ran while one was open for 0% of the time, Pallas kernels for 4%

profile of v5, /device:TPU:8, one launch (start us, length us, event | category | flops | bytes accessed | tf_op | source)
XLA Modules:
  0.0 48.1 jit_solution(11346723776962631934)
XLA Ops:
  0.6 0.0 copy-start.1
  0.6 0.0 copy-start
  0.7 1.9 %project.1 = (bf16[16,1536]{1,0:T(8,128)(2,1)S(1)}, bf16[64,512]{1,0:T(8,128)(2,1)S(1)}, bf16[1024,256]{1,0:T(8,128)(2,1)S(1)}, bf16[2048,256]{1,0:T(8,128)(2,1)S(1)}) custom-call(s32[4]{0:T(128)} %ranks_h.1, s32[2]{0:T(128)} %rows_h.1, bf16[64,1024]{1,0:T(8,128)(2,1)} %bitcast.1, bf16[1024,256]{1,0:T(8,128)(2,1)} %bases_h.1, bf16[16,2048]{1,0:T(8,128)(2,1)} %top_h.1, ...), custom_call_target="tpu_custom_call" | custom-call | flops 50000000 | bytes 1800000 | tf_op jit(solution)/shard_map/project/pallas_call | solution.py:84
  2.6 4.7 %collective-permute-start.6 = (bf16[16,1536]{1,0:T(8,128)(2,1)S(1)}, bf16[16,1536]{1,0:T(8,128)(2,1)S(1)}, u32[]{:S(2)}, u32[]{:S(2)}) collective-permute-start(bf16[16,1536]{1,0:T(8,128)(2,1)S(1)} %get-tuple-element.10.refs_0_), channel_id=1, source_target_pairs={{0,192},{1,193},{2,194},{3,195},{4,196},{5,197},{6,198},{7,199},{8... | collective-permute-start | bytes 147464 | tf_op jit(solution)/shard_map/ppermute | solution.py:32
  7.3 0.0 collective-permute-start.5
  7.3 0.7 %collective-permute-start.4 = (bf16[16,1536]{1,0:T(8,128)(2,1)S(1)}, bf16[16,1536]{1,0:T(8,128)(2,1)S(1)}, u32[]{:S(2)}, u32[]{:S(2)}) collective-permute-start(bf16[16,1536]{1,0:T(8,128)(2,1)S(1)} %get-tuple-element.10.refs_0_), channel_id=1, source_target_pairs={{0,64},{1,65},{2,66},{3,67},{4,68},{5,69},{6,70},{7,71},{8,72},{9,... | collective-permute-start | bytes 147464 | tf_op jit(solution)/shard_map/ppermute | solution.py:32
  8.0 1.8 %collective-permute-done.6.refs_3_ = bf16[16,1536]{1,0:T(8,128)(2,1)S(1)} collective-permute-done((bf16[16,1536]{1,0:T(8,128)(2,1)S(1)}, bf16[16,1536]{1,0:T(8,128)(2,1)S(1)}, u32[]{:S(2)}, u32[]{:S(2)}) %collective-permute-start.6) | collective-permute-done | bytes 49184 | tf_op jit(solution)/shard_map/ppermute | solution.py:32
  9.8 2.5 %collective-permute-done.5.refs_2_ = bf16[16,1536]{1,0:T(8,128)(2,1)S(1)} collective-permute-done((bf16[16,1536]{1,0:T(8,128)(2,1)S(1)}, bf16[16,1536]{1,0:T(8,128)(2,1)S(1)}, u32[]{:S(2)}, u32[]{:S(2)}) %collective-permute-start.5) | collective-permute-done | bytes 49184 | tf_op jit(solution)/shard_map/ppermute | solution.py:32
  12.3 0.0 collective-permute-done.4.refs_1_
  12.3 1.7 %collective-permute-start.9 = (bf16[64,1536]{1,0:T(8,128)(2,1)S(1)}, bf16[64,1536]{1,0:T(8,128)(2,1)S(1)}, u32[]{:S(2)}, u32[]{:S(2)}) collective-permute-start(bf16[64,1536]{1,0:T(8,128)(2,1)S(1)} %shard_map.114.p0), channel_id=1, source_target_pairs={{0,48},{1,49},{2,50},{3,51},{4,52},{5,53},{6,54},{7,55},{8,56},{9,... | collective-permute-start | bytes 589832 | tf_op jit(solution)/shard_map/ppermute | solution.py:32
  14.0 1.0 %collective-permute-start.8 = (bf16[64,1536]{1,0:T(8,128)(2,1)S(1)}, bf16[64,1536]{1,0:T(8,128)(2,1)S(1)}, u32[]{:S(2)}, u32[]{:S(2)}) collective-permute-start(bf16[64,1536]{1,0:T(8,128)(2,1)S(1)} %shard_map.114.p0), channel_id=1, source_target_pairs={{0,32},{1,33},{2,34},{3,35},{4,36},{5,37},{6,38},{7,39},{8,40},{9,... | collective-permute-start | bytes 589832 | tf_op jit(solution)/shard_map/ppermute | solution.py:32
  15.0 1.5 %collective-permute-start.7 = (bf16[64,1536]{1,0:T(8,128)(2,1)S(1)}, bf16[64,1536]{1,0:T(8,128)(2,1)S(1)}, u32[]{:S(2)}, u32[]{:S(2)}) collective-permute-start(bf16[64,1536]{1,0:T(8,128)(2,1)S(1)} %shard_map.114.p0), channel_id=1, source_target_pairs={{0,16},{1,17},{2,18},{3,19},{4,20},{5,21},{6,22},{7,23},{8,24},{9,... | collective-permute-start | bytes 589832 | tf_op jit(solution)/shard_map/ppermute | solution.py:32
  16.5 0.0 collective-permute-start.10
  16.5 5.2 %collective-permute-done.9.p3 = bf16[64,1536]{1,0:T(8,128)(2,1)S(1)} collective-permute-done((bf16[64,1536]{1,0:T(8,128)(2,1)S(1)}, bf16[64,1536]{1,0:T(8,128)(2,1)S(1)}, u32[]{:S(2)}, u32[]{:S(2)}) %collective-permute-start.9) | collective-permute-done | bytes 196640 | tf_op jit(solution)/shard_map/ppermute | solution.py:32
  21.7 0.0 collective-permute-start.13
  21.7 1.5 %collective-permute-done.8.p2 = bf16[64,1536]{1,0:T(8,128)(2,1)S(1)} collective-permute-done((bf16[64,1536]{1,0:T(8,128)(2,1)S(1)}, bf16[64,1536]{1,0:T(8,128)(2,1)S(1)}, u32[]{:S(2)}, u32[]{:S(2)}) %collective-permute-start.8) | collective-permute-done | bytes 196640 | tf_op jit(solution)/shard_map/ppermute | solution.py:32
  23.2 0.0 collective-permute-start.12
  23.2 1.1 %collective-permute-done.7.p1 = bf16[64,1536]{1,0:T(8,128)(2,1)S(1)} collective-permute-done((bf16[64,1536]{1,0:T(8,128)(2,1)S(1)}, bf16[64,1536]{1,0:T(8,128)(2,1)S(1)}, u32[]{:S(2)}, u32[]{:S(2)}) %collective-permute-start.7) | collective-permute-done | bytes 196640 | tf_op jit(solution)/shard_map/ppermute | solution.py:32
  24.3 0.0 collective-permute-start.11
  24.3 6.1 %collective-permute-start = (bf16[64,512]{1,0:T(8,128)(2,1)S(1)}, bf16[64,512]{1,0:T(8,128)(2,1)S(1)}, u32[]{:S(2)}, u32[]{:S(2)}) collective-permute-start(bf16[64,512]{1,0:T(8,128)(2,1)S(1)} %get-tuple-element.8.refs_0_), channel_id=1, source_target_pairs={{0,4},{1,5},{2,6},{3,7},{4,0},{5,1},{6,2},{7,3},{8,12},{9,13},{10,... | collective-permute-start | bytes 196616 | tf_op jit(solution)/shard_map/ppermute | solution.py:32
  30.4 2.8 %collective-permute-done.refs_1_ = bf16[64,512]{1,0:T(8,128)(2,1)S(1)} collective-permute-done((bf16[64,512]{1,0:T(8,128)(2,1)S(1)}, bf16[64,512]{1,0:T(8,128)(2,1)S(1)}, u32[]{:S(2)}, u32[]{:S(2)}) %collective-permute-start) | collective-permute-done | bytes 65568 | tf_op jit(solution)/shard_map/ppermute | solution.py:32
  33.2 1.6 %collective-permute-start.3 = (bf16[128,512]{1,0:T(8,128)(2,1)S(1)}, bf16[128,512]{1,0:T(8,128)(2,1)S(1)}, u32[]{:S(2)}, u32[]{:S(2)}) collective-permute-start(bf16[128,512]{1,0:T(8,128)(2,1)S(1)} %shard_map.113.k0), channel_id=1, source_target_pairs={{0,1},{1,0},{2,3},{3,2},{4,5},{5,4},{6,7},{7,6},{8,9},{9,8},{10,11... | collective-permute-start | bytes 393224 | tf_op jit(solution)/shard_map/ppermute | solution.py:32
  34.8 0.0 collective-permute-done.10.p4
  34.8 2.1 %collective-permute-start.2 = (bf16[128,512]{1,0:T(8,128)(2,1)S(1)}, bf16[128,512]{1,0:T(8,128)(2,1)S(1)}, u32[]{:S(2)}, u32[]{:S(2)}) collective-permute-start(bf16[128,512]{1,0:T(8,128)(2,1)S(1)} %shard_map.113.k0), channel_id=1, source_target_pairs={{0,3},{1,2},{2,1},{3,0},{4,7},{5,6},{6,5},{7,4},{8,11},{9,10},{10,... | collective-permute-start | bytes 393224 | tf_op jit(solution)/shard_map/ppermute | solution.py:32
  36.9 0.0 collective-permute-done.13.p7
  36.9 0.7 %collective-permute-start.1 = (bf16[128,512]{1,0:T(8,128)(2,1)S(1)}, bf16[128,512]{1,0:T(8,128)(2,1)S(1)}, u32[]{:S(2)}, u32[]{:S(2)}) collective-permute-start(bf16[128,512]{1,0:T(8,128)(2,1)S(1)} %shard_map.113.k0), channel_id=1, source_target_pairs={{0,2},{1,3},{2,0},{3,1},{4,6},{5,7},{6,4},{7,5},{8,10},{9,11},{10,... | collective-permute-start | bytes 393224 | tf_op jit(solution)/shard_map/ppermute | solution.py:32
  37.6 1.0 %shard_map.115.inverse = bf16[512,512]{1,0:T(8,128)(2,1)S(1)} custom-call(bf16[512,512]{1,0:T(8,128)(2,1)} %refs_0_.1), custom_call_target="tpu_custom_call" | custom-call | bytes 8000000 | tf_op jit(solution)/shard_map/pallas_call | solution.py:115
  38.7 0.0 collective-permute-done.12.p6
  38.7 0.0 collective-permute-done.11.p5
  38.7 0.6 %solve.1 = (bf16[512,1024]{1,0:T(8,128)(2,1)S(1)}, bf16[512,512]{1,0:T(8,128)(2,1)S(1)}) custom-call(bf16[64,1536]{1,0:T(8,128)(2,1)S(1)} %shard_map.114.p0, bf16[64,1536]{1,0:T(8,128)(2,1)S(1)} %collective-permute-done.7.p1, bf16[64,1536]{1,0:T(8,128)(2,1)S(1)} %collective-permute-done.8.p2, bf16[64,1536]{1,0:T(8,128)(2,1)S(1)} %collective-permute-done.9.p3, ...), custom_call_target="tpu_custom_call" | custom-call | flops 270000000 | bytes 4000000 | tf_op jit(solution)/shard_map/solve/pallas_call | solution.py:183
  39.3 0.0 collective-permute-done.3.k3
  39.3 4.5 %collective-permute-done.2.k2 = bf16[128,512]{1,0:T(8,128)(2,1)S(1)} collective-permute-done((bf16[128,512]{1,0:T(8,128)(2,1)S(1)}, bf16[128,512]{1,0:T(8,128)(2,1)S(1)}, u32[]{:S(2)}, u32[]{:S(2)}) %collective-permute-start.2) | collective-permute-done | bytes 131104 | tf_op jit(solution)/shard_map/ppermute | solution.py:32
  43.9 0.0 collective-permute-done.1.k1
  43.9 0.0 copy-done.1
  43.9 0.0 copy-done
  43.9 4.2 %update.1 = (bf16[1024,2048]{1,0:T(8,128)(2,1)}, bf16[1024,512]{1,0:T(8,128)(2,1)}) custom-call(bf16[128,512]{1,0:T(8,128)(2,1)S(1)} %shard_map.113.k0, bf16[128,512]{1,0:T(8,128)(2,1)S(1)} %collective-permute-done.1.k1, bf16[128,512]{1,0:T(8,128)(2,1)S(1)} %collective-permute-done.2.k2, bf16[128,512]{1,0:T(8,128)(2,1)S(1)} %collective-permute-done.3.k3, ...), custom_call_target="tpu_custom_call" | custom-call | flops 3000000000 | bytes 12000000 | tf_op jit(solution)/shard_map/update/pallas_call | solution.py:226
  (2 shorter events, 0.0 us)
Async XLA Ops:
  0.6 43.2 %copy-start.1 = (bf16[1024,512]{1,0:T(8,128)(2,1)S(1)}, bf16[1024,512]{1,0:T(8,128)(2,1)}, u32[]{:S(2)}) copy-start(bf16[1024,512]{1,0:T(8,128)(2,1)} %rhs.1) | copy-start | bytes 3145732
  0.6 43.2 %copy-start = (bf16[1024,2048]{1,0:T(8,128)(2,1)S(1)}, bf16[1024,2048]{1,0:T(8,128)(2,1)}, u32[]{:S(2)}) copy-start(bf16[1024,2048]{1,0:T(8,128)(2,1)} %slab.1) | copy-start | bytes 12582916
  2.6 7.2 %collective-permute-start.6 = (bf16[16,1536]{1,0:T(8,128)(2,1)S(1)}, bf16[16,1536]{1,0:T(8,128)(2,1)S(1)}, u32[]{:S(2)}, u32[]{:S(2)}) collective-permute-start(bf16[16,1536]{1,0:T(8,128)(2,1)S(1)} %get-tuple-element.10.refs_0_), channel_id=1, source_target_pairs={{0,192},{1,193},{2,194},{3,195},{4,196},{5,197},{6,198},{7,199},{8... | collective-permute-start | bytes 147464 | tf_op jit(solution)/shard_map/ppermute | solution.py:32
  7.3 5.0 %collective-permute-start.5 = (bf16[16,1536]{1,0:T(8,128)(2,1)S(1)}, bf16[16,1536]{1,0:T(8,128)(2,1)S(1)}, u32[]{:S(2)}, u32[]{:S(2)}) collective-permute-start(bf16[16,1536]{1,0:T(8,128)(2,1)S(1)} %get-tuple-element.10.refs_0_), channel_id=1, source_target_pairs={{0,128},{1,129},{2,130},{3,131},{4,132},{5,133},{6,134},{7,135},{8... | collective-permute-start | bytes 147464 | tf_op jit(solution)/shard_map/ppermute | solution.py:32
  7.3 5.0 %collective-permute-start.4 = (bf16[16,1536]{1,0:T(8,128)(2,1)S(1)}, bf16[16,1536]{1,0:T(8,128)(2,1)S(1)}, u32[]{:S(2)}, u32[]{:S(2)}) collective-permute-start(bf16[16,1536]{1,0:T(8,128)(2,1)S(1)} %get-tuple-element.10.refs_0_), channel_id=1, source_target_pairs={{0,64},{1,65},{2,66},{3,67},{4,68},{5,69},{6,70},{7,71},{8,72},{9,... | collective-permute-start | bytes 147464 | tf_op jit(solution)/shard_map/ppermute | solution.py:32
  12.3 9.3 %collective-permute-start.9 = (bf16[64,1536]{1,0:T(8,128)(2,1)S(1)}, bf16[64,1536]{1,0:T(8,128)(2,1)S(1)}, u32[]{:S(2)}, u32[]{:S(2)}) collective-permute-start(bf16[64,1536]{1,0:T(8,128)(2,1)S(1)} %shard_map.114.p0), channel_id=1, source_target_pairs={{0,48},{1,49},{2,50},{3,51},{4,52},{5,53},{6,54},{7,55},{8,56},{9,... | collective-permute-start | bytes 589832 | tf_op jit(solution)/shard_map/ppermute | solution.py:32
  14.0 9.2 %collective-permute-start.8 = (bf16[64,1536]{1,0:T(8,128)(2,1)S(1)}, bf16[64,1536]{1,0:T(8,128)(2,1)S(1)}, u32[]{:S(2)}, u32[]{:S(2)}) collective-permute-start(bf16[64,1536]{1,0:T(8,128)(2,1)S(1)} %shard_map.114.p0), channel_id=1, source_target_pairs={{0,32},{1,33},{2,34},{3,35},{4,36},{5,37},{6,38},{7,39},{8,40},{9,... | collective-permute-start | bytes 589832 | tf_op jit(solution)/shard_map/ppermute | solution.py:32
  15.0 9.3 %collective-permute-start.7 = (bf16[64,1536]{1,0:T(8,128)(2,1)S(1)}, bf16[64,1536]{1,0:T(8,128)(2,1)S(1)}, u32[]{:S(2)}, u32[]{:S(2)}) collective-permute-start(bf16[64,1536]{1,0:T(8,128)(2,1)S(1)} %shard_map.114.p0), channel_id=1, source_target_pairs={{0,16},{1,17},{2,18},{3,19},{4,20},{5,21},{6,22},{7,23},{8,24},{9,... | collective-permute-start | bytes 589832 | tf_op jit(solution)/shard_map/ppermute | solution.py:32
  16.5 18.3 %collective-permute-start.10 = (bf16[64,1536]{1,0:T(8,128)(2,1)S(1)}, bf16[64,1536]{1,0:T(8,128)(2,1)S(1)}, u32[]{:S(2)}, u32[]{:S(2)}) collective-permute-start(bf16[64,1536]{1,0:T(8,128)(2,1)S(1)} %shard_map.114.p0), channel_id=1, source_target_pairs={{0,8},{1,9},{2,10},{3,11},{4,12},{5,13},{6,14},{7,15},{8,0},{9,1},... | collective-permute-start | bytes 589832 | tf_op jit(solution)/shard_map/ppermute | solution.py:32
  21.7 15.2 %collective-permute-start.13 = (bf16[64,1536]{1,0:T(8,128)(2,1)S(1)}, bf16[64,1536]{1,0:T(8,128)(2,1)S(1)}, u32[]{:S(2)}, u32[]{:S(2)}) collective-permute-start(bf16[64,1536]{1,0:T(8,128)(2,1)S(1)} %collective-permute-done.9.p3), channel_id=1, source_target_pairs={{0,8},{1,9},{2,10},{3,11},{4,12},{5,13},{6,14},{7,15},{8,0},{9,1},... | collective-permute-start | bytes 589832 | tf_op jit(solution)/shard_map/ppermute | solution.py:32
  23.2 15.5 %collective-permute-start.12 = (bf16[64,1536]{1,0:T(8,128)(2,1)S(1)}, bf16[64,1536]{1,0:T(8,128)(2,1)S(1)}, u32[]{:S(2)}, u32[]{:S(2)}) collective-permute-start(bf16[64,1536]{1,0:T(8,128)(2,1)S(1)} %collective-permute-done.8.p2), channel_id=1, source_target_pairs={{0,8},{1,9},{2,10},{3,11},{4,12},{5,13},{6,14},{7,15},{8,0},{9,1},... | collective-permute-start | bytes 589832 | tf_op jit(solution)/shard_map/ppermute | solution.py:32
  24.3 14.4 %collective-permute-start.11 = (bf16[64,1536]{1,0:T(8,128)(2,1)S(1)}, bf16[64,1536]{1,0:T(8,128)(2,1)S(1)}, u32[]{:S(2)}, u32[]{:S(2)}) collective-permute-start(bf16[64,1536]{1,0:T(8,128)(2,1)S(1)} %collective-permute-done.7.p1), channel_id=1, source_target_pairs={{0,8},{1,9},{2,10},{3,11},{4,12},{5,13},{6,14},{7,15},{8,0},{9,1},... | collective-permute-start | bytes 589832 | tf_op jit(solution)/shard_map/ppermute | solution.py:32
  24.3 8.9 %collective-permute-start = (bf16[64,512]{1,0:T(8,128)(2,1)S(1)}, bf16[64,512]{1,0:T(8,128)(2,1)S(1)}, u32[]{:S(2)}, u32[]{:S(2)}) collective-permute-start(bf16[64,512]{1,0:T(8,128)(2,1)S(1)} %get-tuple-element.8.refs_0_), channel_id=1, source_target_pairs={{0,4},{1,5},{2,6},{3,7},{4,0},{5,1},{6,2},{7,3},{8,12},{9,13},{10,... | collective-permute-start | bytes 196616 | tf_op jit(solution)/shard_map/ppermute | solution.py:32
  33.2 6.1 %collective-permute-start.3 = (bf16[128,512]{1,0:T(8,128)(2,1)S(1)}, bf16[128,512]{1,0:T(8,128)(2,1)S(1)}, u32[]{:S(2)}, u32[]{:S(2)}) collective-permute-start(bf16[128,512]{1,0:T(8,128)(2,1)S(1)} %shard_map.113.k0), channel_id=1, source_target_pairs={{0,1},{1,0},{2,3},{3,2},{4,5},{5,4},{6,7},{7,6},{8,9},{9,8},{10,11... | collective-permute-start | bytes 393224 | tf_op jit(solution)/shard_map/ppermute | solution.py:32
  34.8 9.1 %collective-permute-start.2 = (bf16[128,512]{1,0:T(8,128)(2,1)S(1)}, bf16[128,512]{1,0:T(8,128)(2,1)S(1)}, u32[]{:S(2)}, u32[]{:S(2)}) collective-permute-start(bf16[128,512]{1,0:T(8,128)(2,1)S(1)} %shard_map.113.k0), channel_id=1, source_target_pairs={{0,3},{1,2},{2,1},{3,0},{4,7},{5,6},{6,5},{7,4},{8,11},{9,10},{10,... | collective-permute-start | bytes 393224 | tf_op jit(solution)/shard_map/ppermute | solution.py:32
  36.9 7.0 %collective-permute-start.1 = (bf16[128,512]{1,0:T(8,128)(2,1)S(1)}, bf16[128,512]{1,0:T(8,128)(2,1)S(1)}, u32[]{:S(2)}, u32[]{:S(2)}) collective-permute-start(bf16[128,512]{1,0:T(8,128)(2,1)S(1)} %shard_map.113.k0), channel_id=1, source_target_pairs={{0,2},{1,3},{2,0},{3,1},{4,6},{5,7},{6,4},{7,5},{8,10},{9,11},{10,... | collective-permute-start | bytes 393224 | tf_op jit(solution)/shard_map/ppermute | solution.py:32
